TPU v7x, 512 devices: a whole 4x8x8 slice. The times are simulated.
512 devices in a mesh: ctx: 32 (over z_hi, y, core), tp: 16 (over z_lo, x).
Axes of the slice: x: 4, y: 8, z: 8 (z_hi: 2, z_lo: 4; z = z_hi * 4 + z_lo), core: 2. Of those that a mesh axis runs over, the one named last changes fastest.
Arguments:
- enc_query: bfloat16 [5120, 6144], P(('ctx', 'tp')), may hold values from -40 to 40
- enc_key: bfloat16 [5120, 6144], P(('ctx', 'tp')), may hold values from -5 to 5
- enc_value: bfloat16 [5120, 6144], P(('ctx', 'tp')), may hold values from -6 to 6
- dec_query: bfloat16 [1024, 6144], P(('ctx', 'tp')), may hold values from -40 to 40
- cross_key: bfloat16 [5120, 6144], P(('ctx', 'tp')), may hold values from -5 to 5
- cross_value: bfloat16 [5120, 6144], P(('ctx', 'tp')), may hold values from -6 to 6
Outputs:
- enc_context: bfloat16 [5120, 6144], P('ctx', 'tp')
- dec_context: bfloat16 [1024, 6144], P('ctx', 'tp')
All inputs are finite; a program needn't handle non-finite values.
Results may differ from a plain program's by a relative error of at most 0.004.
Values may be sent and summed in bfloat16 or wider, within the bound.
A program may use at most 64 MiB of HBM per device.

v0:
```python
import jax
import jax.numpy as jnp
from jax import lax
from jax.sharding import PartitionSpec as P

HEAD_DIM = 128


def shifted(value, axis, steps):
    count = lax.axis_size(axis)
    pairs = [(source, (source + steps) % count) for source in range(count)]
    return lax.ppermute(value, axis, pairs)


def absorb(partial_state, query_block, key_block, value_block):
    row_top, row_total, weighted = partial_state
    head_count = query_block.shape[1] // HEAD_DIM
    query_heads = query_block.reshape(query_block.shape[0], head_count, HEAD_DIM)
    key_heads = key_block.reshape(key_block.shape[0], head_count, HEAD_DIM)
    value_heads = value_block.reshape(value_block.shape[0], head_count, HEAD_DIM)
    scores = jnp.einsum(
        "qhd,khd->hqk", query_heads, key_heads, preferred_element_type=jnp.float32
    ) * HEAD_DIM ** (-0.5)
    new_top = jnp.maximum(row_top, jnp.max(scores, axis=2))
    shrink = jnp.exp(row_top - new_top)
    weights = jnp.exp(scores - new_top[:, :, None])
    row_total = row_total * shrink + jnp.sum(weights, axis=2)
    mixed_values = jnp.einsum(
        "hqk,khd->qhd",
        weights.astype(jnp.bfloat16),
        value_heads,
        preferred_element_type=jnp.float32,
    )
    weighted = weighted * jnp.transpose(shrink)[:, :, None] + mixed_values
    return (new_top, row_total, weighted)


def empty_state(row_count, columns):
    head_count = columns // HEAD_DIM
    return (
        jnp.full((head_count, row_count), -1e30, jnp.float32),
        jnp.zeros((head_count, row_count), jnp.float32),
        jnp.zeros((row_count, head_count, HEAD_DIM), jnp.float32),
    )


def finish(partial_state):
    row_top, row_total, weighted = partial_state
    normed = weighted / jnp.transpose(row_total)[:, :, None]
    return normed.reshape(weighted.shape[0], -1).astype(jnp.bfloat16)


def shards(enc_query, enc_key, enc_value, dec_query, cross_key, cross_value):
    local_query, local_key, local_value, visitor, resident_key, resident_value = (
        lax.all_to_all(enc_query, "tp", split_axis=1, concat_axis=0, tiled=True),
        lax.all_to_all(enc_key, "tp", split_axis=1, concat_axis=0, tiled=True),
        lax.all_to_all(enc_value, "tp", split_axis=1, concat_axis=0, tiled=True),
        lax.all_to_all(dec_query, "tp", split_axis=1, concat_axis=0, tiled=True),
        lax.all_to_all(cross_key, "tp", split_axis=1, concat_axis=0, tiled=True),
        lax.all_to_all(cross_value, "tp", split_axis=1, concat_axis=0, tiled=True),
    )
    enc_state = absorb(
        empty_state(local_query.shape[0], local_query.shape[1]),
        local_query,
        lax.all_gather(local_key, "ctx", axis=0, tiled=True),
        lax.all_gather(local_value, "ctx", axis=0, tiled=True),
    )
    enc_context = finish(enc_state)

    def visit_once(turn_index, loop_carry):
        travel, partial_state = loop_carry
        row_top, row_total, weighted = absorb(partial_state, travel, resident_key, resident_value)
        travel = shifted(travel, "ctx", 1)
        moved = shifted((row_top, row_total, weighted), "ctx", 1)
        return (travel, (moved[0], moved[1], moved[2]))

    travel, dec_state = lax.fori_loop(
        0,
        lax.axis_size("ctx"),
        visit_once,
        (visitor, empty_state(visitor.shape[0], visitor.shape[1])),
    )
    return (enc_context, finish(dec_state))


def solution(mesh):
    in_specs = (
        P(("ctx", "tp"), None),
        P(("ctx", "tp"), None),
        P(("ctx", "tp"), None),
        P(("ctx", "tp"), None),
        P(("ctx", "tp"), None),
        P(("ctx", "tp"), None),
    )
    out_specs = (P("ctx", "tp"), P("ctx", "tp"))
    return jax.shard_map(shards, mesh=mesh, in_specs=in_specs, out_specs=out_specs, check_vma=False)
```

profile of v0, /device:TPU:1, one launch (start us, length us, event | category | flops | bytes accessed | tf_op | source)
XLA Modules:
  0.0 702.3 jit_solution(17084920326577115034)
XLA Ops:
  8.2 18.6 %all_to_all.111 = bf16[10,16,384]{2,0,1:T(8,128)(2,1)S(1)} all-to-all(bf16[10,16,384]{2,0,1:T(8,128)(2,1)S(1)} %copy.19), channel_id=1, replica_groups=mesh['ctx'=32,'tp'=16] {'tp'}, dimensions={1} | all-to-all | bytes 245760 | tf_op jit(solution)/shard_map/all_to_all | solution.py:56
  27.5 4.4 all-to-all-start.3
  33.6 5.2 all-to-all-done.3
  44.1 6.6 all-to-all-done
  55.9 6.6 all-to-all-done.2
  67.7 6.6 all-to-all-done.4
  78.7 7.4 %all-to-all-done.5 = bf16[10,16,384]{2,0,1:T(8,128)(2,1)S(1)} async-done(((bf16[10,16,384]{2,0,1:T(8,128)(2,1)}), bf16[10,16,384]{2,0,1:T(8,128)(2,1)S(1)}, u32[]{:S(2)}, u32[]{:S(2)}) %all-to-all-start.5) | async-done | bytes 122912 | tf_op jit(solution)/shard_map/all_to_all | solution.py:60
  86.2 579.2 %while.16 = (s32[]{:T(128)}, bf16[32,384]{1,0:T(8,128)(2,1)S(1)}, f32[3,32]{1,0:T(4,128)S(1)}, f32[3,32]{1,0:T(4,128)S(1)}, f32[32,3,128]{2,0,1:T(8,128)S(1)}, /...) while((s32[]{:T(128)}, bf16[32,384]{1,0:T(8,128)(2,1)S(1)}, ...), condition=%wide.region_5.0_spmd, body=%wide.region_2.0_spmd.sunk | while | flops 7981346 | bytes 906485 | solution.py:77
  86.2 30.6 %collective-permute-start = (bf16[32,384]{1,0:T(8,128)(2,1)S(1)}, bf16[32,384]{1,0:T(8,128)(2,1)S(1)}, u32[]{:S(2)}, u32[]{:S(2)}) collective-permute-start(bf16[32,384]{1,0:T(8,128)(2,1)S(1)} %copy.78), channel_id=1, source_target_pairs={{0,16},{16,32},{32,48},{48,64},{64,80},{80,96},{96,112},{112,128},... | collective-permute-start | bytes 73736 | tf_op jit(solution)/shard_map/while/body/eval_jaxpr/ppermute | solution.py:12
  167.7 4.7 collective-permute-done.1
  172.5 4.3 collective-permute-done.2
  185.2 4.7 collective-permute-done.1
  202.6 4.8 collective-permute-done.1
  220.2 5.1 collective-permute-done.1
  225.3 4.3 collective-permute-done.2
  238.0 4.7 collective-permute-done.1
  242.7 4.3 collective-permute-done.2
  255.4 4.7 collective-permute-done.1
  272.9 4.7 collective-permute-done.1
  277.6 4.3 collective-permute-done.2
  290.3 4.7 collective-permute-done.1
  295.0 4.3 collective-permute-done.2
  307.7 4.7 collective-permute-done.1
  325.2 4.7 collective-permute-done.1
  342.6 4.7 collective-permute-done.1
  347.3 4.3 collective-permute-done.2
  360.0 4.7 collective-permute-done.1
  377.5 4.7 collective-permute-done.1
  394.9 4.7 collective-permute-done.1
  412.3 4.7 collective-permute-done.1
  417.1 4.3 collective-permute-done.2
  429.8 4.7 collective-permute-done.1
  447.2 4.7 collective-permute-done.1
  464.6 4.7 collective-permute-done.1
  482.1 4.7 collective-permute-done.1
  499.5 4.7 collective-permute-done.1
  516.9 4.7 collective-permute-done.1
  534.4 4.7 collective-permute-done.1
  551.8 4.7 collective-permute-done.1
  569.2 4.7 collective-permute-done.1
  586.7 4.7 collective-permute-done.1
  604.1 4.7 collective-permute-done.1
  621.5 4.7 collective-permute-done.1
  639.0 4.7 collective-permute-done.1
  656.4 4.7 collective-permute-done.1
  666.1 6.3 copy.20
  681.6 6.3 copy.24
  687.9 6.9 fusion.30
  (485 shorter events, 413.5 us)
Async XLA Ops:
  7.2 658.9 %all-gather.3.cloned.1.call-start = ((), (), s32[]{:S(2)}) async-start(), calls=%async_computation.6 | async-start | bytes 4055040 | tf_op jit(solution)/shard_map/all_gather | solution.py:65
  77.8 603.8 %all-gather.5.cloned.1.call-start = ((), (), s32[]{:S(2)}) async-start(), calls=%async_computation.7 | async-start | bytes 4055040 | tf_op jit(solution)/shard_map/all_gather | solution.py:66
  86.2 39.8 %collective-permute-start = (bf16[32,384]{1,0:T(8,128)(2,1)S(1)}, bf16[32,384]{1,0:T(8,128)(2,1)S(1)}, u32[]{:S(2)}, u32[]{:S(2)}) collective-permute-start(bf16[32,384]{1,0:T(8,128)(2,1)S(1)} %copy.78), channel_id=1, source_target_pairs={{0,16},{16,32},{32,48},{48,64},{64,80},{80,96},{96,112},{112,128},... | collective-permute-start | bytes 73736 | tf_op jit(solution)/shard_map/while/body/eval_jaxpr/ppermute | solution.py:12
  126.0 15.8 %collective-permute-start = (bf16[32,384]{1,0:T(8,128)(2,1)S(1)}, bf16[32,384]{1,0:T(8,128)(2,1)S(1)}, u32[]{:S(2)}, u32[]{:S(2)}) collective-permute-start(bf16[32,384]{1,0:T(8,128)(2,1)S(1)} %copy.78), channel_id=1, source_target_pairs={{0,16},{16,32},{32,48},{48,64},{64,80},{80,96},{96,112},{112,128},... | collective-permute-start | bytes 73736 | tf_op jit(solution)/shard_map/while/body/eval_jaxpr/ppermute | solution.py:12
  141.9 17.4 %collective-permute-start = (bf16[32,384]{1,0:T(8,128)(2,1)S(1)}, bf16[32,384]{1,0:T(8,128)(2,1)S(1)}, u32[]{:S(2)}, u32[]{:S(2)}) collective-permute-start(bf16[32,384]{1,0:T(8,128)(2,1)S(1)} %copy.78), channel_id=1, source_target_pairs={{0,16},{16,32},{32,48},{48,64},{64,80},{80,96},{96,112},{112,128},... | collective-permute-start | bytes 73736 | tf_op jit(solution)/shard_map/while/body/eval_jaxpr/ppermute | solution.py:12
  146.3 13.1 %collective-permute-start.3 = (f32[32,3,128]{2,0,1:T(8,128)S(1)}, f32[32,3,128]{2,0,1:T(8,128)S(1)}, u32[]{:S(2)}, u32[]{:S(2)}) collective-permute-start(f32[32,3,128]{2,0,1:T(8,128)S(1)} %fusion.61), channel_id=1, source_target_pairs={{0,16},{16,32},{32,48},{48,64},{64,80},{80,96},{96,112},{112,128},... | collective-permute-start | bytes 147464 | tf_op jit(solution)/shard_map/while/body/eval_jaxpr/ppermute | solution.py:12
  159.3 17.4 %collective-permute-start = (bf16[32,384]{1,0:T(8,128)(2,1)S(1)}, bf16[32,384]{1,0:T(8,128)(2,1)S(1)}, u32[]{:S(2)}, u32[]{:S(2)}) collective-permute-start(bf16[32,384]{1,0:T(8,128)(2,1)S(1)} %copy.78), channel_id=1, source_target_pairs={{0,16},{16,32},{32,48},{48,64},{64,80},{80,96},{96,112},{112,128},... | collective-permute-start | bytes 73736 | tf_op jit(solution)/shard_map/while/body/eval_jaxpr/ppermute | solution.py:12
  176.7 17.4 %collective-permute-start = (bf16[32,384]{1,0:T(8,128)(2,1)S(1)}, bf16[32,384]{1,0:T(8,128)(2,1)S(1)}, u32[]{:S(2)}, u32[]{:S(2)}) collective-permute-start(bf16[32,384]{1,0:T(8,128)(2,1)S(1)} %copy.78), channel_id=1, source_target_pairs={{0,16},{16,32},{32,48},{48,64},{64,80},{80,96},{96,112},{112,128},... | collective-permute-start | bytes 73736 | tf_op jit(solution)/shard_map/while/body/eval_jaxpr/ppermute | solution.py:12
  181.1 13.1 %collective-permute-start.3 = (f32[32,3,128]{2,0,1:T(8,128)S(1)}, f32[32,3,128]{2,0,1:T(8,128)S(1)}, u32[]{:S(2)}, u32[]{:S(2)}) collective-permute-start(f32[32,3,128]{2,0,1:T(8,128)S(1)} %fusion.61), channel_id=1, source_target_pairs={{0,16},{16,32},{32,48},{48,64},{64,80},{80,96},{96,112},{112,128},... | collective-permute-start | bytes 147464 | tf_op jit(solution)/shard_map/while/body/eval_jaxpr/ppermute | solution.py:12
  194.2 17.5 %collective-permute-start = (bf16[32,384]{1,0:T(8,128)(2,1)S(1)}, bf16[32,384]{1,0:T(8,128)(2,1)S(1)}, u32[]{:S(2)}, u32[]{:S(2)}) collective-permute-start(bf16[32,384]{1,0:T(8,128)(2,1)S(1)} %copy.78), channel_id=1, source_target_pairs={{0,16},{16,32},{32,48},{48,64},{64,80},{80,96},{96,112},{112,128},... | collective-permute-start | bytes 73736 | tf_op jit(solution)/shard_map/while/body/eval_jaxpr/ppermute | solution.py:12
  198.6 13.2 %collective-permute-start.3 = (f32[32,3,128]{2,0,1:T(8,128)S(1)}, f32[32,3,128]{2,0,1:T(8,128)S(1)}, u32[]{:S(2)}, u32[]{:S(2)}) collective-permute-start(f32[32,3,128]{2,0,1:T(8,128)S(1)} %fusion.61), channel_id=1, source_target_pairs={{0,16},{16,32},{32,48},{48,64},{64,80},{80,96},{96,112},{112,128},... | collective-permute-start | bytes 147464 | tf_op jit(solution)/shard_map/while/body/eval_jaxpr/ppermute | solution.py:12
  211.7 17.8 %collective-permute-start = (bf16[32,384]{1,0:T(8,128)(2,1)S(1)}, bf16[32,384]{1,0:T(8,128)(2,1)S(1)}, u32[]{:S(2)}, u32[]{:S(2)}) collective-permute-start(bf16[32,384]{1,0:T(8,128)(2,1)S(1)} %copy.78), channel_id=1, source_target_pairs={{0,16},{16,32},{32,48},{48,64},{64,80},{80,96},{96,112},{112,128},... | collective-permute-start | bytes 73736 | tf_op jit(solution)/shard_map/while/body/eval_jaxpr/ppermute | solution.py:12
  216.1 13.5 %collective-permute-start.3 = (f32[32,3,128]{2,0,1:T(8,128)S(1)}, f32[32,3,128]{2,0,1:T(8,128)S(1)}, u32[]{:S(2)}, u32[]{:S(2)}) collective-permute-start(f32[32,3,128]{2,0,1:T(8,128)S(1)} %fusion.61), channel_id=1, source_target_pairs={{0,16},{16,32},{32,48},{48,64},{64,80},{80,96},{96,112},{112,128},... | collective-permute-start | bytes 147464 | tf_op jit(solution)/shard_map/while/body/eval_jaxpr/ppermute | solution.py:12
  229.6 17.4 %collective-permute-start = (bf16[32,384]{1,0:T(8,128)(2,1)S(1)}, bf16[32,384]{1,0:T(8,128)(2,1)S(1)}, u32[]{:S(2)}, u32[]{:S(2)}) collective-permute-start(bf16[32,384]{1,0:T(8,128)(2,1)S(1)} %copy.78), channel_id=1, source_target_pairs={{0,16},{16,32},{32,48},{48,64},{64,80},{80,96},{96,112},{112,128},... | collective-permute-start | bytes 73736 | tf_op jit(solution)/shard_map/while/body/eval_jaxpr/ppermute | solution.py:12
  247.0 17.4 %collective-permute-start = (bf16[32,384]{1,0:T(8,128)(2,1)S(1)}, bf16[32,384]{1,0:T(8,128)(2,1)S(1)}, u32[]{:S(2)}, u32[]{:S(2)}) collective-permute-start(bf16[32,384]{1,0:T(8,128)(2,1)S(1)} %copy.78), channel_id=1, source_target_pairs={{0,16},{16,32},{32,48},{48,64},{64,80},{80,96},{96,112},{112,128},... | collective-permute-start | bytes 73736 | tf_op jit(solution)/shard_map/while/body/eval_jaxpr/ppermute | solution.py:12
  251.4 13.1 %collective-permute-start.3 = (f32[32,3,128]{2,0,1:T(8,128)S(1)}, f32[32,3,128]{2,0,1:T(8,128)S(1)}, u32[]{:S(2)}, u32[]{:S(2)}) collective-permute-start(f32[32,3,128]{2,0,1:T(8,128)S(1)} %fusion.61), channel_id=1, source_target_pairs={{0,16},{16,32},{32,48},{48,64},{64,80},{80,96},{96,112},{112,128},... | collective-permute-start | bytes 147464 | tf_op jit(solution)/shard_map/while/body/eval_jaxpr/ppermute | solution.py:12
  264.4 17.4 %collective-permute-start = (bf16[32,384]{1,0:T(8,128)(2,1)S(1)}, bf16[32,384]{1,0:T(8,128)(2,1)S(1)}, u32[]{:S(2)}, u32[]{:S(2)}) collective-permute-start(bf16[32,384]{1,0:T(8,128)(2,1)S(1)} %copy.78), channel_id=1, source_target_pairs={{0,16},{16,32},{32,48},{48,64},{64,80},{80,96},{96,112},{112,128},... | collective-permute-start | bytes 73736 | tf_op jit(solution)/shard_map/while/body/eval_jaxpr/ppermute | solution.py:12
  268.8 13.1 %collective-permute-start.3 = (f32[32,3,128]{2,0,1:T(8,128)S(1)}, f32[32,3,128]{2,0,1:T(8,128)S(1)}, u32[]{:S(2)}, u32[]{:S(2)}) collective-permute-start(f32[32,3,128]{2,0,1:T(8,128)S(1)} %fusion.61), channel_id=1, source_target_pairs={{0,16},{16,32},{32,48},{48,64},{64,80},{80,96},{96,112},{112,128},... | collective-permute-start | bytes 147464 | tf_op jit(solution)/shard_map/while/body/eval_jaxpr/ppermute | solution.py:12
  281.9 17.4 %collective-permute-start = (bf16[32,384]{1,0:T(8,128)(2,1)S(1)}, bf16[32,384]{1,0:T(8,128)(2,1)S(1)}, u32[]{:S(2)}, u32[]{:S(2)}) collective-permute-start(bf16[32,384]{1,0:T(8,128)(2,1)S(1)} %copy.78), channel_id=1, source_target_pairs={{0,16},{16,32},{32,48},{48,64},{64,80},{80,96},{96,112},{112,128},... | collective-permute-start | bytes 73736 | tf_op jit(solution)/shard_map/while/body/eval_jaxpr/ppermute | solution.py:12
  299.3 17.4 %collective-permute-start = (bf16[32,384]{1,0:T(8,128)(2,1)S(1)}, bf16[32,384]{1,0:T(8,128)(2,1)S(1)}, u32[]{:S(2)}, u32[]{:S(2)}) collective-permute-start(bf16[32,384]{1,0:T(8,128)(2,1)S(1)} %copy.78), channel_id=1, source_target_pairs={{0,16},{16,32},{32,48},{48,64},{64,80},{80,96},{96,112},{112,128},... | collective-permute-start | bytes 73736 | tf_op jit(solution)/shard_map/while/body/eval_jaxpr/ppermute | solution.py:12
  303.7 13.1 %collective-permute-start.3 = (f32[32,3,128]{2,0,1:T(8,128)S(1)}, f32[32,3,128]{2,0,1:T(8,128)S(1)}, u32[]{:S(2)}, u32[]{:S(2)}) collective-permute-start(f32[32,3,128]{2,0,1:T(8,128)S(1)} %fusion.61), channel_id=1, source_target_pairs={{0,16},{16,32},{32,48},{48,64},{64,80},{80,96},{96,112},{112,128},... | collective-permute-start | bytes 147464 | tf_op jit(solution)/shard_map/while/body/eval_jaxpr/ppermute | solution.py:12
  316.7 17.4 %collective-permute-start = (bf16[32,384]{1,0:T(8,128)(2,1)S(1)}, bf16[32,384]{1,0:T(8,128)(2,1)S(1)}, u32[]{:S(2)}, u32[]{:S(2)}) collective-permute-start(bf16[32,384]{1,0:T(8,128)(2,1)S(1)} %copy.78), channel_id=1, source_target_pairs={{0,16},{16,32},{32,48},{48,64},{64,80},{80,96},{96,112},{112,128},... | collective-permute-start | bytes 73736 | tf_op jit(solution)/shard_map/while/body/eval_jaxpr/ppermute | solution.py:12
  321.1 13.1 %collective-permute-start.3 = (f32[32,3,128]{2,0,1:T(8,128)S(1)}, f32[32,3,128]{2,0,1:T(8,128)S(1)}, u32[]{:S(2)}, u32[]{:S(2)}) collective-permute-start(f32[32,3,128]{2,0,1:T(8,128)S(1)} %fusion.61), channel_id=1, source_target_pairs={{0,16},{16,32},{32,48},{48,64},{64,80},{80,96},{96,112},{112,128},... | collective-permute-start | bytes 147464 | tf_op jit(solution)/shard_map/while/body/eval_jaxpr/ppermute | solution.py:12
  334.2 17.4 %collective-permute-start = (bf16[32,384]{1,0:T(8,128)(2,1)S(1)}, bf16[32,384]{1,0:T(8,128)(2,1)S(1)}, u32[]{:S(2)}, u32[]{:S(2)}) collective-permute-start(bf16[32,384]{1,0:T(8,128)(2,1)S(1)} %copy.78), channel_id=1, source_target_pairs={{0,16},{16,32},{32,48},{48,64},{64,80},{80,96},{96,112},{112,128},... | collective-permute-start | bytes 73736 | tf_op jit(solution)/shard_map/while/body/eval_jaxpr/ppermute | solution.py:12
  351.6 17.4 %collective-permute-start = (bf16[32,384]{1,0:T(8,128)(2,1)S(1)}, bf16[32,384]{1,0:T(8,128)(2,1)S(1)}, u32[]{:S(2)}, u32[]{:S(2)}) collective-permute-start(bf16[32,384]{1,0:T(8,128)(2,1)S(1)} %copy.78), channel_id=1, source_target_pairs={{0,16},{16,32},{32,48},{48,64},{64,80},{80,96},{96,112},{112,128},... | collective-permute-start | bytes 73736 | tf_op jit(solution)/shard_map/while/body/eval_jaxpr/ppermute | solution.py:12
  356.0 13.1 %collective-permute-start.3 = (f32[32,3,128]{2,0,1:T(8,128)S(1)}, f32[32,3,128]{2,0,1:T(8,128)S(1)}, u32[]{:S(2)}, u32[]{:S(2)}) collective-permute-start(f32[32,3,128]{2,0,1:T(8,128)S(1)} %fusion.61), channel_id=1, source_target_pairs={{0,16},{16,32},{32,48},{48,64},{64,80},{80,96},{96,112},{112,128},... | collective-permute-start | bytes 147464 | tf_op jit(solution)/shard_map/while/body/eval_jaxpr/ppermute | solution.py:12
  369.0 17.4 %collective-permute-start = (bf16[32,384]{1,0:T(8,128)(2,1)S(1)}, bf16[32,384]{1,0:T(8,128)(2,1)S(1)}, u32[]{:S(2)}, u32[]{:S(2)}) collective-permute-start(bf16[32,384]{1,0:T(8,128)(2,1)S(1)} %copy.78), channel_id=1, source_target_pairs={{0,16},{16,32},{32,48},{48,64},{64,80},{80,96},{96,112},{112,128},... | collective-permute-start | bytes 73736 | tf_op jit(solution)/shard_map/while/body/eval_jaxpr/ppermute | solution.py:12
  373.4 13.1 %collective-permute-start.3 = (f32[32,3,128]{2,0,1:T(8,128)S(1)}, f32[32,3,128]{2,0,1:T(8,128)S(1)}, u32[]{:S(2)}, u32[]{:S(2)}) collective-permute-start(f32[32,3,128]{2,0,1:T(8,128)S(1)} %fusion.61), channel_id=1, source_target_pairs={{0,16},{16,32},{32,48},{48,64},{64,80},{80,96},{96,112},{112,128},... | collective-permute-start | bytes 147464 | tf_op jit(solution)/shard_map/while/body/eval_jaxpr/ppermute | solution.py:12
  386.5 17.4 %collective-permute-start = (bf16[32,384]{1,0:T(8,128)(2,1)S(1)}, bf16[32,384]{1,0:T(8,128)(2,1)S(1)}, u32[]{:S(2)}, u32[]{:S(2)}) collective-permute-start(bf16[32,384]{1,0:T(8,128)(2,1)S(1)} %copy.78), channel_id=1, source_target_pairs={{0,16},{16,32},{32,48},{48,64},{64,80},{80,96},{96,112},{112,128},... | collective-permute-start | bytes 73736 | tf_op jit(solution)/shard_map/while/body/eval_jaxpr/ppermute | solution.py:12
  403.9 17.4 %collective-permute-start = (bf16[32,384]{1,0:T(8,128)(2,1)S(1)}, bf16[32,384]{1,0:T(8,128)(2,1)S(1)}, u32[]{:S(2)}, u32[]{:S(2)}) collective-permute-start(bf16[32,384]{1,0:T(8,128)(2,1)S(1)} %copy.78), channel_id=1, source_target_pairs={{0,16},{16,32},{32,48},{48,64},{64,80},{80,96},{96,112},{112,128},... | collective-permute-start | bytes 73736 | tf_op jit(solution)/shard_map/while/body/eval_jaxpr/ppermute | solution.py:12
  408.3 13.1 %collective-permute-start.3 = (f32[32,3,128]{2,0,1:T(8,128)S(1)}, f32[32,3,128]{2,0,1:T(8,128)S(1)}, u32[]{:S(2)}, u32[]{:S(2)}) collective-permute-start(f32[32,3,128]{2,0,1:T(8,128)S(1)} %fusion.61), channel_id=1, source_target_pairs={{0,16},{16,32},{32,48},{48,64},{64,80},{80,96},{96,112},{112,128},... | collective-permute-start | bytes 147464 | tf_op jit(solution)/shard_map/while/body/eval_jaxpr/ppermute | solution.py:12
  421.3 17.4 %collective-permute-start = (bf16[32,384]{1,0:T(8,128)(2,1)S(1)}, bf16[32,384]{1,0:T(8,128)(2,1)S(1)}, u32[]{:S(2)}, u32[]{:S(2)}) collective-permute-start(bf16[32,384]{1,0:T(8,128)(2,1)S(1)} %copy.78), channel_id=1, source_target_pairs={{0,16},{16,32},{32,48},{48,64},{64,80},{80,96},{96,112},{112,128},... | collective-permute-start | bytes 73736 | tf_op jit(solution)/shard_map/while/body/eval_jaxpr/ppermute | solution.py:12
  425.7 13.1 %collective-permute-start.3 = (f32[32,3,128]{2,0,1:T(8,128)S(1)}, f32[32,3,128]{2,0,1:T(8,128)S(1)}, u32[]{:S(2)}, u32[]{:S(2)}) collective-permute-start(f32[32,3,128]{2,0,1:T(8,128)S(1)} %fusion.61), channel_id=1, source_target_pairs={{0,16},{16,32},{32,48},{48,64},{64,80},{80,96},{96,112},{112,128},... | collective-permute-start | bytes 147464 | tf_op jit(solution)/shard_map/while/body/eval_jaxpr/ppermute | solution.py:12
  438.8 17.4 %collective-permute-start = (bf16[32,384]{1,0:T(8,128)(2,1)S(1)}, bf16[32,384]{1,0:T(8,128)(2,1)S(1)}, u32[]{:S(2)}, u32[]{:S(2)}) collective-permute-start(bf16[32,384]{1,0:T(8,128)(2,1)S(1)} %copy.78), channel_id=1, source_target_pairs={{0,16},{16,32},{32,48},{48,64},{64,80},{80,96},{96,112},{112,128},... | collective-permute-start | bytes 73736 | tf_op jit(solution)/shard_map/while/body/eval_jaxpr/ppermute | solution.py:12
  456.2 17.4 %collective-permute-start = (bf16[32,384]{1,0:T(8,128)(2,1)S(1)}, bf16[32,384]{1,0:T(8,128)(2,1)S(1)}, u32[]{:S(2)}, u32[]{:S(2)}) collective-permute-start(bf16[32,384]{1,0:T(8,128)(2,1)S(1)} %copy.78), channel_id=1, source_target_pairs={{0,16},{16,32},{32,48},{48,64},{64,80},{80,96},{96,112},{112,128},... | collective-permute-start | bytes 73736 | tf_op jit(solution)/shard_map/while/body/eval_jaxpr/ppermute | solution.py:12
  460.6 13.1 %collective-permute-start.3 = (f32[32,3,128]{2,0,1:T(8,128)S(1)}, f32[32,3,128]{2,0,1:T(8,128)S(1)}, u32[]{:S(2)}, u32[]{:S(2)}) collective-permute-start(f32[32,3,128]{2,0,1:T(8,128)S(1)} %fusion.61), channel_id=1, source_target_pairs={{0,16},{16,32},{32,48},{48,64},{64,80},{80,96},{96,112},{112,128},... | collective-permute-start | bytes 147464 | tf_op jit(solution)/shard_map/while/body/eval_jaxpr/ppermute | solution.py:12
  473.6 17.4 %collective-permute-start = (bf16[32,384]{1,0:T(8,128)(2,1)S(1)}, bf16[32,384]{1,0:T(8,128)(2,1)S(1)}, u32[]{:S(2)}, u32[]{:S(2)}) collective-permute-start(bf16[32,384]{1,0:T(8,128)(2,1)S(1)} %copy.78), channel_id=1, source_target_pairs={{0,16},{16,32},{32,48},{48,64},{64,80},{80,96},{96,112},{112,128},... | collective-permute-start | bytes 73736 | tf_op jit(solution)/shard_map/while/body/eval_jaxpr/ppermute | solution.py:12
  491.1 17.4 %collective-permute-start = (bf16[32,384]{1,0:T(8,128)(2,1)S(1)}, bf16[32,384]{1,0:T(8,128)(2,1)S(1)}, u32[]{:S(2)}, u32[]{:S(2)}) collective-permute-start(bf16[32,384]{1,0:T(8,128)(2,1)S(1)} %copy.78), channel_id=1, source_target_pairs={{0,16},{16,32},{32,48},{48,64},{64,80},{80,96},{96,112},{112,128},... | collective-permute-start | bytes 73736 | tf_op jit(solution)/shard_map/while/body/eval_jaxpr/ppermute | solution.py:12
  508.5 17.4 %collective-permute-start = (bf16[32,384]{1,0:T(8,128)(2,1)S(1)}, bf16[32,384]{1,0:T(8,128)(2,1)S(1)}, u32[]{:S(2)}, u32[]{:S(2)}) collective-permute-start(bf16[32,384]{1,0:T(8,128)(2,1)S(1)} %copy.78), channel_id=1, source_target_pairs={{0,16},{16,32},{32,48},{48,64},{64,80},{80,96},{96,112},{112,128},... | collective-permute-start | bytes 73736 | tf_op jit(solution)/shard_map/while/body/eval_jaxpr/ppermute | solution.py:12
  512.9 13.1 %collective-permute-start.3 = (f32[32,3,128]{2,0,1:T(8,128)S(1)}, f32[32,3,128]{2,0,1:T(8,128)S(1)}, u32[]{:S(2)}, u32[]{:S(2)}) collective-permute-start(f32[32,3,128]{2,0,1:T(8,128)S(1)} %fusion.61), channel_id=1, source_target_pairs={{0,16},{16,32},{32,48},{48,64},{64,80},{80,96},{96,112},{112,128},... | collective-permute-start | bytes 147464 | tf_op jit(solution)/shard_map/while/body/eval_jaxpr/ppermute | solution.py:12
  525.9 17.4 %collective-permute-start = (bf16[32,384]{1,0:T(8,128)(2,1)S(1)}, bf16[32,384]{1,0:T(8,128)(2,1)S(1)}, u32[]{:S(2)}, u32[]{:S(2)}) collective-permute-start(bf16[32,384]{1,0:T(8,128)(2,1)S(1)} %copy.78), channel_id=1, source_target_pairs={{0,16},{16,32},{32,48},{48,64},{64,80},{80,96},{96,112},{112,128},... | collective-permute-start | bytes 73736 | tf_op jit(solution)/shard_map/while/body/eval_jaxpr/ppermute | solution.py:12
  543.4 17.4 %collective-permute-start = (bf16[32,384]{1,0:T(8,128)(2,1)S(1)}, bf16[32,384]{1,0:T(8,128)(2,1)S(1)}, u32[]{:S(2)}, u32[]{:S(2)}) collective-permute-start(bf16[32,384]{1,0:T(8,128)(2,1)S(1)} %copy.78), channel_id=1, source_target_pairs={{0,16},{16,32},{32,48},{48,64},{64,80},{80,96},{96,112},{112,128},... | collective-permute-start | bytes 73736 | tf_op jit(solution)/shard_map/while/body/eval_jaxpr/ppermute | solution.py:12
  560.8 17.4 %collective-permute-start = (bf16[32,384]{1,0:T(8,128)(2,1)S(1)}, bf16[32,384]{1,0:T(8,128)(2,1)S(1)}, u32[]{:S(2)}, u32[]{:S(2)}) collective-permute-start(bf16[32,384]{1,0:T(8,128)(2,1)S(1)} %copy.78), channel_id=1, source_target_pairs={{0,16},{16,32},{32,48},{48,64},{64,80},{80,96},{96,112},{112,128},... | collective-permute-start | bytes 73736 | tf_op jit(solution)/shard_map/while/body/eval_jaxpr/ppermute | solution.py:12
  578.2 17.4 %collective-permute-start = (bf16[32,384]{1,0:T(8,128)(2,1)S(1)}, bf16[32,384]{1,0:T(8,128)(2,1)S(1)}, u32[]{:S(2)}, u32[]{:S(2)}) collective-permute-start(bf16[32,384]{1,0:T(8,128)(2,1)S(1)} %copy.78), channel_id=1, source_target_pairs={{0,16},{16,32},{32,48},{48,64},{64,80},{80,96},{96,112},{112,128},... | collective-permute-start | bytes 73736 | tf_op jit(solution)/shard_map/while/body/eval_jaxpr/ppermute | solution.py:12
  595.7 17.4 %collective-permute-start = (bf16[32,384]{1,0:T(8,128)(2,1)S(1)}, bf16[32,384]{1,0:T(8,128)(2,1)S(1)}, u32[]{:S(2)}, u32[]{:S(2)}) collective-permute-start(bf16[32,384]{1,0:T(8,128)(2,1)S(1)} %copy.78), channel_id=1, source_target_pairs={{0,16},{16,32},{32,48},{48,64},{64,80},{80,96},{96,112},{112,128},... | collective-permute-start | bytes 73736 | tf_op jit(solution)/shard_map/while/body/eval_jaxpr/ppermute | solution.py:12
  613.1 17.4 %collective-permute-start = (bf16[32,384]{1,0:T(8,128)(2,1)S(1)}, bf16[32,384]{1,0:T(8,128)(2,1)S(1)}, u32[]{:S(2)}, u32[]{:S(2)}) collective-permute-start(bf16[32,384]{1,0:T(8,128)(2,1)S(1)} %copy.78), channel_id=1, source_target_pairs={{0,16},{16,32},{32,48},{48,64},{64,80},{80,96},{96,112},{112,128},... | collective-permute-start | bytes 73736 | tf_op jit(solution)/shard_map/while/body/eval_jaxpr/ppermute | solution.py:12
  630.6 17.4 %collective-permute-start = (bf16[32,384]{1,0:T(8,128)(2,1)S(1)}, bf16[32,384]{1,0:T(8,128)(2,1)S(1)}, u32[]{:S(2)}, u32[]{:S(2)}) collective-permute-start(bf16[32,384]{1,0:T(8,128)(2,1)S(1)} %copy.78), channel_id=1, source_target_pairs={{0,16},{16,32},{32,48},{48,64},{64,80},{80,96},{96,112},{112,128},... | collective-permute-start | bytes 73736 | tf_op jit(solution)/shard_map/while/body/eval_jaxpr/ppermute | solution.py:12
  648.0 17.4 %collective-permute-start = (bf16[32,384]{1,0:T(8,128)(2,1)S(1)}, bf16[32,384]{1,0:T(8,128)(2,1)S(1)}, u32[]{:S(2)}, u32[]{:S(2)}) collective-permute-start(bf16[32,384]{1,0:T(8,128)(2,1)S(1)} %copy.78), channel_id=1, source_target_pairs={{0,16},{16,32},{32,48},{48,64},{64,80},{80,96},{96,112},{112,128},... | collective-permute-start | bytes 73736 | tf_op jit(solution)/shard_map/while/body/eval_jaxpr/ppermute | solution.py:12
  (88 other events, 966.8 us)
Sparse Core Ops, SparseCore 0:
  27.7 108.5 all-gather.2
  140.2 100.9 all-gather.4
where the time goes:
time: 713 us; the launch traced here: 702 us
  waiting for transfers between devices  305 us (43%)
  starting transfers between devices  301 us (42%)
  matrix products  26.7 us (4%)
  local copies, waits for them, and re-layouts  26.4 us (4%)
  blocking collectives  18.6 us (3%)
  between operations  14.2 us (2%)
  other arithmetic  8.55 us (1%)
    ppermute x128, starting transfers between devices, shifted(): return lax.ppermute(value, axis, pairs)  282 us
    ppermute x128, waiting for transfers between devices, shifted(): return lax.ppermute(value, axis, pairs)  273 us
    all_to_all x1, blocking collectives, shards(): lax.all_to_all(enc_key, 'tp', split_axis=1, concat_axis=0, tiled=True)  18.6 us
  transfers between devices with their start and end apart: 135, of which 67 were waited for; matrix products, arithmetic and copies ran while one was open for 6% of the time, Pallas kernels for 0%

commit v1 on v0

--- a/solution.py
+++ b/solution.py
@@ -4,12 +4,6 @@
 from jax.sharding import PartitionSpec as P
 
 HEAD_DIM = 128
-
-
-def shifted(value, axis, steps):
-    count = lax.axis_size(axis)
-    pairs = [(source, (source + steps) % count) for source in range(count)]
-    return lax.ppermute(value, axis, pairs)
 
 
 def absorb(partial_state, query_block, key_block, value_block):
@@ -67,20 +61,24 @@
     )
     enc_context = finish(enc_state)
 
-    def visit_once(turn_index, loop_carry):
-        travel, partial_state = loop_carry
-        row_top, row_total, weighted = absorb(partial_state, travel, resident_key, resident_value)
-        travel = shifted(travel, "ctx", 1)
-        moved = shifted((row_top, row_total, weighted), "ctx", 1)
-        return (travel, (moved[0], moved[1], moved[2]))
-
-    travel, dec_state = lax.fori_loop(
-        0,
-        lax.axis_size("ctx"),
-        visit_once,
-        (visitor, empty_state(visitor.shape[0], visitor.shape[1])),
+    ring = lax.axis_size("ctx")
+    rows, columns = visitor.shape
+    heads = columns // HEAD_DIM
+    every_query = lax.all_gather(visitor, "ctx", axis=0, tiled=True)
+    row_top, row_total, weighted = absorb(
+        empty_state(rows * ring, columns), every_query, resident_key, resident_value
     )
-    return (enc_context, finish(dec_state))
+    stats = jnp.stack([row_top.T, row_total.T], axis=1).reshape(ring, rows, 2 * heads)
+    sums = weighted.reshape(ring, rows, columns).astype(jnp.bfloat16)
+    stats = lax.all_to_all(stats, "ctx", split_axis=0, concat_axis=0, tiled=True)
+    sums = lax.all_to_all(sums, "ctx", split_axis=0, concat_axis=0, tiled=True)
+    stats = stats.reshape(ring, rows, 2, heads)
+    tops, totals = stats[:, :, 0], stats[:, :, 1]
+    scale = jnp.exp(tops - jnp.max(tops, axis=0, keepdims=True))
+    total = jnp.sum(scale * totals, axis=0)
+    mixed = jnp.sum(scale[..., None] * sums.reshape(ring, rows, heads, HEAD_DIM).astype(jnp.float32), axis=0)
+    dec_context = (mixed / total[..., None]).reshape(rows, columns).astype(jnp.bfloat16)
+    return (enc_context, dec_context)
 
 
 def solution(mesh):

time: 713 us -> 266 us (0.37); the launches traced: 702 us -> 265 us
  starting transfers between devices: 301 us -> 28.6 us
  waiting for transfers between devices: 305 us -> 81.7 us
  blocking collectives: 18.6 us -> 92.9 us
  matrix products: 26.7 us -> 12 us
    ppermute x128 -> x0, starting transfers between devices: 282 us -> none  [shifted(): return lax.ppermute(value, axis, pairs)]
    ppermute x128 -> x0, waiting for transfers between devices: 273 us -> none  [shifted(): return lax.ppermute(value, axis, pairs)]
    all_gather x0 -> x1, blocking collectives: none -> 61.8 us  [shards(): every_query = lax.all_gather(visitor, 'ctx', axis=0, tiled=True)]
    all_gather x1, waiting for transfers between devices: 0.02 us -> 33.3 us  [shards(): lax.all_gather(local_value, 'ctx', axis=0, tiled=True)]
    all_to_all x1 -> x2, waiting for transfers between devices: 6.58 us -> 29.2 us  [the longest x1 20.3 us: shards(): sums = lax.all_to_all(sums, 'ctx', split_axis=0, concat_axis=0, tiled=True)]
    all_to_all x0 -> x1, blocking collectives: none -> 12.5 us  [shards(): lax.all_to_all(enc_value, 'tp', split_axis=1, concat_axis=0, tiled=True)]
    dot_general x33 -> x2, matrix products: 12.8 us -> 4.07 us  [absorb(): jnp.einsum('qhd,khd->hqk', query_heads, key_heads, preferred_element_type...]
  transfers between devices with their start and end apart: 135 -> 8, of which waited for: 67 -> 6; matrix products, arithmetic and copies ran while one was open for 6% -> 11% of each run, Pallas kernels for 0% -> 0%
where the time goes in v1:
time: 266 us; the launch traced here: 265 us
  blocking collectives  92.9 us (35%)
  waiting for transfers between devices  81.7 us (31%)
  local copies, waits for them, and re-layouts  30.2 us (11%)
  starting transfers between devices  28.6 us (11%)
  between operations  14.3 us (5%)
  matrix products  12 us (5%)
  other arithmetic  5.18 us (2%)
    all_gather x1, blocking collectives, shards(): every_query = lax.all_gather(visitor, 'ctx', axis=0, tiled=True)  61.8 us
    all_gather x1, waiting for transfers between devices, shards(): lax.all_gather(local_value, 'ctx', axis=0, tiled=True)  33.3 us
    all_to_all x1, waiting for transfers between devices, shards(): sums = lax.all_to_all(sums, 'ctx', split_axis=0, concat_axis=0, tiled=True)  20.3 us
    all_to_all x1, blocking collectives, shards(): lax.all_to_all(enc_key, 'tp', split_axis=1, concat_axis=0, tiled=True)  18.6 us
    all_to_all x1, blocking collectives, shards(): lax.all_to_all(enc_value, 'tp', split_axis=1, concat_axis=0, tiled=True)  12.5 us
    all_to_all x1, waiting for transfers between devices, shards(): lax.all_to_all(stats, 'ctx', split_axis=0, concat_axis=0, tiled=True)  8.81 us
    all_to_all x1, waiting for transfers between devices, shards(): lax.all_to_all(cross_value, 'tp', split_axis=1, concat_axis=0, tiled=True)  8.13 us
    dot_general x2, matrix products, absorb(): jnp.einsum('hqk,khd->qhd', weights.astype(jnp.bfloat16), value_heads, pre...  7.91 us
  transfers between devices with their start and end apart: 8, of which 6 were waited for; matrix products, arithmetic and copies ran while one was open for 11% of the time, Pallas kernels for 0%

profile of v1, /device:TPU:1, one launch (start us, length us, event | category | flops | bytes accessed | tf_op | source)
XLA Modules:
  0.0 264.9 jit_solution(9463373634563402771)
XLA Ops:
  7.2 1.0 copy.75
  8.3 18.6 %all_to_all.115 = bf16[10,16,384]{2,0,1:T(8,128)(2,1)S(1)} all-to-all(bf16[10,16,384]{2,0,1:T(8,128)(2,1)S(1)} %copy.50), channel_id=1, replica_groups=mesh['ctx'=32,'tp'=16] {'tp'}, dimensions={1} | all-to-all | bytes 245760 | tf_op jit(solution)/shard_map/all_to_all | solution.py:50
  26.9 0.7 all_to_all.90
  27.7 1.0 copy.76
  28.7 12.5 %all_to_all.116 = bf16[10,16,384]{2,0,1:T(8,128)(2,1)S(1)} all-to-all(bf16[10,16,384]{2,0,1:T(8,128)(2,1)S(1)} %copy.54), channel_id=1, replica_groups=mesh['ctx'=32,'tp'=16] {'tp'}, dimensions={1} | all-to-all | bytes 245760 | tf_op jit(solution)/shard_map/all_to_all | solution.py:51
  41.2 0.7 all_to_all.94
  41.9 4.2 %all-to-all-start.3 = ((bf16[2,16,384]{2,0,1:T(2,128)(2,1)}), bf16[2,16,384]{2,0,1:T(2,128)(2,1)S(1)}, u32[]{:S(2)}, u32[]{:S(2)}) async-start(bf16[2,16,384]{2,0,1:T(2,128)(2,1)} %bitcast.118), calls=%async_computation.3 | async-start | bytes 49152 | tf_op jit(solution)/shard_map/all_to_all | solution.py:52
  46.1 1.0 copy.77
  47.1 0.7 copy.60
  47.8 0.7 copy.66
  48.6 0.7 copy.49
  49.3 3.8 %all-to-all-done.3 = bf16[2,16,384]{2,0,1:T(2,128)(2,1)S(1)} async-done(((bf16[2,16,384]{2,0,1:T(2,128)(2,1)}), bf16[2,16,384]{2,0,1:T(2,128)(2,1)S(1)}, u32[]{:S(2)}, u32[]{:S(2)}) %all-to-all-start.3) | async-done | bytes 24608 | tf_op jit(solution)/shard_map/all_to_all | solution.py:52
  53.1 3.5 %all-to-all-start.4 = ((bf16[10,16,384]{2,0,1:T(8,128)(2,1)}), bf16[10,16,384]{2,0,1:T(8,128)(2,1)S(1)}, u32[]{:S(2)}, u32[]{:S(2)}) async-start(bf16[10,16,384]{2,0,1:T(8,128)(2,1)} %copy.60), calls=%async_computation.4 | async-start | bytes 393216 | tf_op jit(solution)/shard_map/all_to_all | solution.py:53
  56.7 61.8 %all_gather.11 = bf16[1024,384]{1,0:T(8,128)(2,1)S(1)} all-gather(bf16[32,384]{1,0:T(8,128)(2,1)S(1)} %all_to_all.98), channel_id=1, replica_groups=mesh['ctx'=32,'tp'=16] {'ctx'}, dimensions={0}, use_global_device_ids=true | all-gather | bytes 811008 | tf_op jit(solution)/shard_map/all_gather | solution.py:67
  118.5 0.3 copy.59
  118.8 6.6 %all-to-all-start.6 = ((bf16[10,16,384]{2,0,1:T(8,128)(2,1)}), bf16[10,16,384]{2,0,1:T(8,128)(2,1)S(1)}, u32[]{:S(2)}, u32[]{:S(2)}) async-start(bf16[10,16,384]{2,0,1:T(8,128)(2,1)} %copy.66), calls=%async_computation.6 | async-start | bytes 393216 | tf_op jit(solution)/shard_map/all_to_all | solution.py:54
  125.5 0.4 multiply_reduce_fusion.1
  125.9 0.4 fusion.7
  126.3 8.1 %all-to-all-done.6 = bf16[10,16,384]{2,0,1:T(8,128)(2,1)S(1)} async-done(((bf16[10,16,384]{2,0,1:T(8,128)(2,1)}), bf16[10,16,384]{2,0,1:T(8,128)(2,1)S(1)}, u32[]{:S(2)}, u32[]{:S(2)}) %all-to-all-start.6) | async-done | bytes 122912 | tf_op jit(solution)/shard_map/all_to_all | solution.py:54
  134.4 3.9 %all-to-all-start = ((bf16[10,16,384]{2,0,1:T(8,128)(2,1)}), bf16[10,16,384]{2,0,1:T(8,128)(2,1)S(1)}, u32[]{:S(2)}, u32[]{:S(2)}) async-start(bf16[10,16,384]{2,0,1:T(8,128)(2,1)} %copy.49), calls=%async_computation | async-start | bytes 393216 | tf_op jit(solution)/shard_map/all_to_all | solution.py:49
  138.3 0.1 reshape.82
  138.5 0.7 reshape.85
  139.3 7.3 %all-to-all-done = bf16[10,16,384]{2,0,1:T(8,128)(2,1)S(1)} async-done(((bf16[10,16,384]{2,0,1:T(8,128)(2,1)}), bf16[10,16,384]{2,0,1:T(8,128)(2,1)S(1)}, u32[]{:S(2)}, u32[]{:S(2)}) %all-to-all-start) | async-done | bytes 122912 | tf_op jit(solution)/shard_map/all_to_all | solution.py:49
  146.6 5.8 %all-to-all-start.5 = ((f32[32,1,192]{2,1,0:T(1,128)}), f32[32,1,192]{2,1,0:T(1,128)S(1)}, u32[]{:S(2)}, u32[]{:S(2)}) async-start(f32[32,1,192]{2,1,0:T(1,128)} %reshape.85), calls=%async_computation.5 | async-start | bytes 65536 | tf_op jit(solution)/shard_map/all_to_all | solution.py:73
  152.4 1.0 fusion.8
  153.4 0.7 copy.68
  154.1 1.4 convert_element_type.30
  155.5 8.8 %all-to-all-done.5 = f32[32,1,192]{2,1,0:T(1,128)S(1)} async-done(((f32[32,1,192]{2,1,0:T(1,128)}), f32[32,1,192]{2,1,0:T(1,128)S(1)}, u32[]{:S(2)}, u32[]{:S(2)}) %all-to-all-start.5) | async-done | bytes 24608 | tf_op jit(solution)/shard_map/all_to_all | solution.py:73
  164.3 4.6 %all-to-all-start.7 = ((bf16[32,32,384]{2,1,0:T(8,128)(2,1)}), bf16[32,32,384]{2,1,0:T(8,128)(2,1)S(1)}, u32[]{:S(2)}, u32[]{:S(2)}) async-start(bf16[32,32,384]{2,1,0:T(8,128)(2,1)} %convert_element_type.30), calls=%async_computation.7 | async-start | bytes 1572864 | tf_op jit(solution)/shard_map/all_to_all | solution.py:74
  168.9 0.7 reshape.77
  169.7 0.5 broadcast.36
  170.2 0.7 reduce.2
  171.1 0.3 copy.65
  171.4 1.2 mul.41
  172.6 1.8 mul.42
  174.4 0.1 copy.69
  174.5 20.3 %all-to-all-done.7 = bf16[32,32,384]{2,1,0:T(8,128)(2,1)S(1)} async-done(((bf16[32,32,384]{2,1,0:T(8,128)(2,1)}), bf16[32,32,384]{2,1,0:T(8,128)(2,1)S(1)}, u32[]{:S(2)}, u32[]{:S(2)}) %all-to-all-start.7) | async-done | bytes 786464 | tf_op jit(solution)/shard_map/all_to_all | solution.py:74
  194.8 1.6 multiply_reduce_fusion.2
  196.4 0.1 div.21
  196.5 0.6 fusion.32
  197.1 6.3 %copy.51 = bf16[5120,384]{0,1:T(8,128)(2,1)} copy(bf16[5120,384]{1,0:T(8,128)(2,1)} %all-gather.3.cloned.1.call-done) | data formatting | bytes 7864320 | tf_op jit(solution)/shard_map/all_gather | solution.py:59
  203.4 3.6 %multiply_reduce_fusion = (f32[3,160]{1,0:T(4,128)S(1)}, f32[3,160,5120]{2,1,0:T(8,128)S(1)}) fusion(bf16[5120,3,128]{0,2,1:T(8,128)(2,1)} %bitcast.93, bf16[160,3,128]{2,1,0:T(4,128)(2,1)S(1)} %copy-done.1), kind=kOutput, calls=%fused_computation.1 | convolution fusion | flops 634060288 | bytes 13887360 | tf_op jit(solution)/shard_map/qhd,khd->hqk/dot_general | solution.py:15
  207.1 1.8 fusion
  208.9 2.0 copy-done
  210.9 33.3 %all-gather.5.cloned.1.call-done = bf16[5120,384]{1,0:T(8,128)(2,1)} async-done(((bf16[160,384]{1,0:T(8,128)(2,1)}), bf16[5120,384]{1,0:T(8,128)(2,1)}) %all-gather.5.cloned.1.call-update) | async-done | bytes 3932176 | tf_op jit(solution)/shard_map/all_gather | solution.py:60
  244.2 6.3 %copy.55 = bf16[5120,384]{0,1:T(8,128)(2,1)} copy(bf16[5120,384]{1,0:T(8,128)(2,1)} %all-gather.5.cloned.1.call-done) | data formatting | bytes 7864320 | tf_op jit(solution)/shard_map/all_gather | solution.py:60
  250.5 6.9 %fusion.21 = bf16[3,20,8,128]{3,2,1,0:T(8,128)(2,1)S(1)} fusion(bf16[5120,3,128]{0,2,1:T(8,128)(2,1)} %bitcast.94, f32[3,160,5120]{2,1,0:T(8,128)} %copy-done, f32[3,160]{1,0:T(4,128)S(1)} %get-tuple-element.9, f32[160,3]{0,1:T(4,128)S(1)} %bitcast_add_fusion.2, f32[160,3]{0,1:T(4,128)S(1)} %get-tuple-element.8), kind=kOutput, calls=%fused_computation.18 | convolution fusion | flops 636702720 | bytes 13891200 | tf_op jit(solution)/shard_map/hqk,khd->qhd/dot_general | solution.py:22
  257.4 0.7 copy.93
  (35 shorter events, 0.7 us)
Async XLA Ops:
  7.2 40.6 %copy-start.2 = (bf16[10,6144]{1,0:T(8,128)(2,1)S(1)}, bf16[10,6144]{1,0:T(8,128)(2,1)}, u32[]{:S(2)}) copy-start(bf16[10,6144]{1,0:T(8,128)(2,1)} %param.11) | copy-start | bytes 368644
  7.2 41.4 %copy-start.3 = (bf16[10,6144]{1,0:T(8,128)(2,1)S(1)}, bf16[10,6144]{1,0:T(8,128)(2,1)}, u32[]{:S(2)}) copy-start(bf16[10,6144]{1,0:T(8,128)(2,1)} %param.6) | copy-start | bytes 368644
  7.2 189.9 %all-gather.3.cloned.1.call-start = ((), (), s32[]{:S(2)}) async-start(), calls=%async_computation.8 | async-start | bytes 4055040 | tf_op jit(solution)/shard_map/all_gather | solution.py:59
  27.7 216.5 %all-gather.5.cloned.1.call-start = ((), (), s32[]{:S(2)}) async-start(), calls=%async_computation.9 | async-start | bytes 4055040 | tf_op jit(solution)/shard_map/all_gather | solution.py:60
  41.9 11.2 %all-to-all-start.3 = ((bf16[2,16,384]{2,0,1:T(2,128)(2,1)}), bf16[2,16,384]{2,0,1:T(2,128)(2,1)S(1)}, u32[]{:S(2)}, u32[]{:S(2)}) async-start(bf16[2,16,384]{2,0,1:T(2,128)(2,1)} %bitcast.118), calls=%async_computation.3 | async-start | bytes 49152 | tf_op jit(solution)/shard_map/all_to_all | solution.py:52
  53.1 65.7 %all-to-all-start.4 = ((bf16[10,16,384]{2,0,1:T(8,128)(2,1)}), bf16[10,16,384]{2,0,1:T(8,128)(2,1)S(1)}, u32[]{:S(2)}, u32[]{:S(2)}) async-start(bf16[10,16,384]{2,0,1:T(8,128)(2,1)} %copy.60), calls=%async_computation.4 | async-start | bytes 393216 | tf_op jit(solution)/shard_map/all_to_all | solution.py:53
  118.8 15.6 %all-to-all-start.6 = ((bf16[10,16,384]{2,0,1:T(8,128)(2,1)}), bf16[10,16,384]{2,0,1:T(8,128)(2,1)S(1)}, u32[]{:S(2)}, u32[]{:S(2)}) async-start(bf16[10,16,384]{2,0,1:T(8,128)(2,1)} %copy.66), calls=%async_computation.6 | async-start | bytes 393216 | tf_op jit(solution)/shard_map/all_to_all | solution.py:54
  134.4 12.2 %all-to-all-start = ((bf16[10,16,384]{2,0,1:T(8,128)(2,1)}), bf16[10,16,384]{2,0,1:T(8,128)(2,1)S(1)}, u32[]{:S(2)}, u32[]{:S(2)}) async-start(bf16[10,16,384]{2,0,1:T(8,128)(2,1)} %copy.49), calls=%async_computation | async-start | bytes 393216 | tf_op jit(solution)/shard_map/all_to_all | solution.py:49
  146.6 17.8 %all-to-all-start.5 = ((f32[32,1,192]{2,1,0:T(1,128)}), f32[32,1,192]{2,1,0:T(1,128)S(1)}, u32[]{:S(2)}, u32[]{:S(2)}) async-start(f32[32,1,192]{2,1,0:T(1,128)} %reshape.85), calls=%async_computation.5 | async-start | bytes 65536 | tf_op jit(solution)/shard_map/all_to_all | solution.py:73
  164.3 30.5 %all-to-all-start.7 = ((bf16[32,32,384]{2,1,0:T(8,128)(2,1)}), bf16[32,32,384]{2,1,0:T(8,128)(2,1)S(1)}, u32[]{:S(2)}, u32[]{:S(2)}) async-start(bf16[32,32,384]{2,1,0:T(8,128)(2,1)} %convert_element_type.30), calls=%async_computation.7 | async-start | bytes 1572864 | tf_op jit(solution)/shard_map/all_to_all | solution.py:74
  197.1 6.3 %copy-start.1 = (bf16[160,3,128]{2,1,0:T(4,128)(2,1)S(1)}, bf16[160,3,128]{2,1,0:T(4,128)(2,1)}, u32[]{:S(2)}) copy-start(bf16[160,3,128]{2,1,0:T(4,128)(2,1)} %reshape.77) | copy-start | bytes 368644
  207.1 3.8 %copy-start = (f32[3,160,5120]{2,1,0:T(8,128)}, f32[3,160,5120]{2,1,0:T(8,128)S(1)}, u32[]{:S(2)}) copy-start(f32[3,160,5120]{2,1,0:T(8,128)S(1)} %get-tuple-element.11) | copy-start | bytes 29491204
Sparse Core Ops, SparseCore 0:
  27.8 109.4 all-gather.2
  141.2 102.8 all-gather.4

commit v2 on v0

v2 whole, which is shorter than its diff:
```python
import functools

import jax
import jax.numpy as jnp
from jax import lax
from jax.experimental import pallas as pl
from jax.experimental.pallas import tpu as pltpu
from jax.sharding import PartitionSpec as P

HEAD_DIM = 128
RING = 8
LOG2E = 1.4426950408889634
STEEP = HEAD_DIM ** (-0.5) * LOG2E
MESH = pl.DeviceIdType.MESH
KEY_RIGHT = (1, 2, 3, 4)
VALUE_RIGHT = (1, 2, 3)


def scores_of(query, key):
    return lax.dot_general(query, key, (((1,), (1,)), ((), ())), preferred_element_type=jnp.float32)


def kernel(
    q_ref, k_ref, v_ref, dq_ref, ck_ref, cv_ref, enc_ref, dec_ref,
    qb, kb, vb, db, ckb, cvb, top, total, acc, estat, dstat,
    esend, esend_stat, eback, eback_stat, psend, psend_stat, pback, pback_stat,
    wide, zsend, zsend_stat, zback, zback_stat, dmix,
    ks, kr, vs, vr, ds, dr, kps, kpr, vps, vpr, rs, rr, rts, rtr, ms, mr, local,
):
    rows, columns = q_ref.shape
    drows = dq_ref.shape[0]
    heads = columns // HEAD_DIM
    me = lax.axis_index("ctx")
    plane, y, core = me // (2 * RING), (me // 2) % RING, me % 2

    def along(offset):
        return {"ctx": plane * (2 * RING) + lax.rem(y + offset + RING, RING) * 2 + core}

    twin = {"ctx": plane * (2 * RING) + y * 2 + (1 - core)}
    mirror = {"ctx": (1 - plane) * (2 * RING) + y * 2 + core}

    barrier = pltpu.get_barrier_semaphore()
    for peer in [along(offset) for offset in range(1, RING)] + [twin, mirror]:
        pl.semaphore_signal(barrier, inc=1, device_id=peer, device_id_type=MESH)
    pl.semaphore_wait(barrier, RING + 1)

    started = []

    def send(source, target, send_sem, recv_sem, device):
        copy = pltpu.make_async_remote_copy(
            src_ref=source, dst_ref=target, send_sem=send_sem, recv_sem=recv_sem,
            device_id=device, device_id_type=MESH,
        )
        copy.start()
        started.append(copy)

    def arrived(target, recv_sem):
        pltpu.make_async_remote_copy(
            src_ref=target, dst_ref=target, send_sem=recv_sem, recv_sem=recv_sem,
            device_id=twin, device_id_type=MESH,
        ).wait_recv()

    def onward(source, slot, buffer, send_sems, recv_sems, right):
        after, before = (slot + 1) % RING, (slot - 1) % RING
        if after in right:
            send(source, buffer(after), send_sems.at[after], recv_sems.at[after], along(1))
        if before not in right and before != 0:
            send(source, buffer(before), send_sems.at[before], recv_sems.at[before], along(-1))

    def pass_on(source, slot, buffer, send_sems, recv_sems, right):
        if slot == 0:
            onward(source, 0, buffer, send_sems, recv_sems, right)
        elif slot in right:
            if slot + 1 in right:
                send(source, buffer(slot + 1), send_sems.at[slot + 1], recv_sems.at[slot + 1], along(1))
        elif slot - 1 not in right and slot - 1 != 0:
            send(source, buffer(slot - 1), send_sems.at[slot - 1], recv_sems.at[slot - 1], along(-1))

    def key_slot(slot):
        return kb.at[slot, 0]

    def value_slot(slot):
        return vb.at[slot, 0]

    def query_slot(slot):
        return db.at[slot]

    send(dq_ref, db.at[0, 1], ms.at[0], mr.at[0], mirror)
    pass_on(k_ref, 0, key_slot, ks, kr, KEY_RIGHT)
    pass_on(v_ref, 0, value_slot, vs, vr, VALUE_RIGHT)
    send(k_ref, kb.at[0, 1], kps.at[0], kpr.at[0], twin)
    send(v_ref, vb.at[0, 1], vps.at[0], vpr.at[0], twin)
    send(q_ref, qb.at[1], ms.at[1], mr.at[1], mirror)
    send(ck_ref, ckb.at[1], ms.at[2], mr.at[2], twin)
    send(cv_ref, cvb.at[1], ms.at[3], mr.at[3], twin)
    own = pltpu.make_async_copy(dq_ref, db.at[0, 0], local)
    own.start()
    kb[0, 0] = k_ref[...]
    vb[0, 0] = v_ref[...]
    qb[0] = q_ref[...]
    ckb[0] = ck_ref[...]
    cvb[0] = cv_ref[...]
    own.wait()
    arrived(db.at[0, 1], mr.at[0])
    pass_on(db.at[0], 0, query_slot, ds, dr, KEY_RIGHT)
    estat[...] = jnp.zeros_like(estat)
    dstat[...] = jnp.zeros_like(dstat)
    wide[...] = jnp.zeros_like(wide)

    def attend(slots, first):
        def body(item, carry):
            half, head = item // heads, item % heads
            at = pl.ds(pl.multiple_of(head * HEAD_DIM, HEAD_DIM), HEAD_DIM)
            query = qb[half, :, at]
            parts = [scores_of(query, kb[slot, :, :, at].reshape(2 * rows, HEAD_DIM)) for slot in slots]
            new_top = functools.reduce(jnp.maximum, [jnp.max(part, axis=1, keepdims=True) for part in parts])
            if not first:
                new_top = jnp.maximum(new_top, top[item])
            mixed, summed = None, None
            for slot, part in zip(slots, parts):
                weights = jnp.exp2((part - new_top) * STEEP)
                one = jnp.sum(weights, axis=1, keepdims=True)
                two = jnp.dot(
                    weights.astype(jnp.bfloat16),
                    vb[slot, :, :, at].reshape(2 * rows, HEAD_DIM),
                    preferred_element_type=jnp.float32,
                )
                summed = one if summed is None else summed + one
                mixed = two if mixed is None else mixed + two
            if not first:
                shrink = jnp.exp2((top[item] - new_top) * STEEP)
                summed = summed + total[item] * shrink
                mixed = mixed + acc[item] * shrink
            top[item] = new_top
            total[item] = summed
            acc[item] = mixed
            return carry

        lax.fori_loop(0, 2 * heads, body, 0)

    def visit(slot):
        def body(head, carry):
            at = pl.ds(pl.multiple_of(head * HEAD_DIM, HEAD_DIM), HEAD_DIM)
            query = db[slot, :, :, at].reshape(2 * drows, HEAD_DIM)
            part = scores_of(query, ckb[:, :, at].reshape(2 * rows, HEAD_DIM))
            row_top = jnp.max(part, axis=1, keepdims=True)
            weights = jnp.exp2((part - row_top) * STEEP)
            summed = jnp.sum(weights, axis=1, keepdims=True)
            mixed = jnp.dot(
                weights.astype(jnp.bfloat16), cvb[:, :, at].reshape(2 * rows, HEAD_DIM),
                preferred_element_type=jnp.float32,
            )
            psend[slot, :, at] = mixed.astype(jnp.bfloat16)
            lane = lax.broadcasted_iota(jnp.int32, (2 * drows, HEAD_DIM), 1)
            held = dstat[0 : 2 * drows, :]
            held = jnp.where(lane == head, row_top, held)
            dstat[0 : 2 * drows, :] = jnp.where(lane == heads + head, summed, held)
            return carry

        lax.fori_loop(0, heads, body, 0)
        psend_stat[slot] = jnp.transpose(dstat[...])[0:8]
        if slot > 0:
            send(psend.at[slot], pback.at[slot], rs.at[slot], rr.at[slot], along(-slot))
            send(psend_stat.at[slot], pback_stat.at[slot], rts.at[slot], rtr.at[slot], along(-slot))
        else:
            pback[0] = psend[0]
            pback_stat[0] = psend_stat[0]

    arrived(kb.at[0, 1], kpr.at[0])
    arrived(vb.at[0, 1], vpr.at[0])
    arrived(qb.at[1], mr.at[1])
    attend((0,), True)
    arrived(ckb.at[1], mr.at[2])
    arrived(cvb.at[1], mr.at[3])
    visit(0)

    for step in range(1, RING // 2 + 1):
        pair = (step,) if step == RING - step else (step, RING - step)
        for slot in pair:
            arrived(kb.at[slot, 0], kr.at[slot])
            pass_on(kb.at[slot, 0], slot, key_slot, ks, kr, KEY_RIGHT)
            send(kb.at[slot, 0], kb.at[slot, 1], kps.at[slot], kpr.at[slot], twin)
        for slot in pair:
            arrived(vb.at[slot, 0], vr.at[slot])
            pass_on(vb.at[slot, 0], slot, value_slot, vs, vr, VALUE_RIGHT)
            send(vb.at[slot, 0], vb.at[slot, 1], vps.at[slot], vpr.at[slot], twin)
        for slot in pair:
            arrived(db.at[slot], dr.at[slot])
            pass_on(db.at[slot], slot, query_slot, ds, dr, KEY_RIGHT)
        for slot in pair:
            visit(slot)
        for slot in pair:
            arrived(kb.at[slot, 1], kpr.at[slot])
            arrived(vb.at[slot, 1], vpr.at[slot])
        attend(pair, False)

    lane = lax.broadcasted_iota(jnp.int32, (rows, HEAD_DIM), 1)
    held = jnp.zeros((rows, HEAD_DIM), jnp.float32)
    for head in range(heads):
        item = heads + head
        esend[:, head * HEAD_DIM : (head + 1) * HEAD_DIM] = acc[item].astype(jnp.bfloat16)
        held = jnp.where(lane == head, top[item], held)
        held = jnp.where(lane == heads + head, total[item], held)
    estat[0:rows, :] = held
    for chunk in range(2):
        esend_stat[chunk] = jnp.transpose(estat[chunk * 128 : (chunk + 1) * 128, :])[0:8]
    send(esend, eback, ms.at[4], mr.at[4], mirror)
    send(esend_stat, eback_stat, ms.at[5], mr.at[5], mirror)

    for slot in range(1, RING):
        arrived(pback.at[slot], rr.at[slot])
        arrived(pback_stat.at[slot], rtr.at[slot])
    stats = [pback_stat[slot] for slot in range(RING)]
    best = functools.reduce(jnp.maximum, [stat[0:heads] for stat in stats])
    joined = None
    for slot in range(RING):
        weight = jnp.exp2((stats[slot][0:heads] - best) * STEEP)
        wide[slot * 8 : slot * 8 + heads, :] = weight
        term = weight * stats[slot][heads : 2 * heads]
        joined = term if joined is None else joined + term
    zsend_stat[...] = jnp.zeros_like(zsend_stat)
    zsend_stat[0:heads, :] = best
    zsend_stat[heads : 2 * heads, :] = joined
    turned = jnp.transpose(wide[...])
    for head in range(heads):
        span = slice(head * HEAD_DIM, (head + 1) * HEAD_DIM)
        mixed = None
        for slot in range(RING):
            term = pback[slot, :, span].astype(jnp.float32) * turned[0 : 2 * drows, slot * 8 + head : slot * 8 + head + 1]
            mixed = term if mixed is None else mixed + term
        dmix[:, span] = mixed
        zsend[:, span] = mixed[drows:].astype(jnp.bfloat16)
    send(zsend, zback, ms.at[6], mr.at[6], mirror)
    send(zsend_stat, zback_stat, ms.at[7], mr.at[7], mirror)

    arrived(eback, mr.at[4])
    arrived(eback_stat, mr.at[5])
    wide[8:, :] = jnp.zeros((120, 128), jnp.float32)
    for chunk in range(2):
        wide[0:8, :] = eback_stat[chunk]
        estat[chunk * 128 : (chunk + 1) * 128, :] = jnp.transpose(wide[...])
    for head in range(heads):
        span = slice(head * HEAD_DIM, (head + 1) * HEAD_DIM)
        other_top = estat[0:rows, head : head + 1]
        other_total = estat[0:rows, heads + head : heads + head + 1]
        peak = jnp.maximum(top[head], other_top)
        mine = jnp.exp2((top[head] - peak) * STEEP)
        theirs = jnp.exp2((other_top - peak) * STEEP)
        whole = mine * acc[head] + theirs * eback[:, span].astype(jnp.float32)
        enc_ref[:, span] = (whole / (mine * total[head] + theirs * other_total)).astype(jnp.bfloat16)

    arrived(zback, mr.at[6])
    arrived(zback_stat, mr.at[7])
    wide[0:8, :] = zsend_stat[...]
    wide[8:16, :] = zback_stat[...]
    turned = jnp.transpose(wide[...])
    for head in range(heads):
        span = slice(head * HEAD_DIM, (head + 1) * HEAD_DIM)
        own_top = turned[0:drows, head : head + 1]
        own_total = turned[0:drows, heads + head : heads + head + 1]
        other_top = turned[drows : 2 * drows, 8 + head : 8 + head + 1]
        other_total = turned[drows : 2 * drows, 8 + heads + head : 8 + heads + head + 1]
        peak = jnp.maximum(own_top, other_top)
        mine = jnp.exp2((own_top - peak) * STEEP)
        theirs = jnp.exp2((other_top - peak) * STEEP)
        whole = mine * dmix[0:drows, span] + theirs * zback[:, span].astype(jnp.float32)
        dec_ref[:, span] = (whole / (mine * own_total + theirs * other_total)).astype(jnp.bfloat16)

    for copy in started:
        copy.wait_send()


def attention(query, key, value, dec_query, cross_key, cross_value):
    rows, columns = query.shape
    drows = dec_query.shape[0]
    heads = columns // HEAD_DIM
    bf16, f32 = jnp.bfloat16, jnp.float32
    vmem = pl.BlockSpec(memory_space=pltpu.VMEM)
    eight = pltpu.SemaphoreType.DMA((RING,))
    return pl.pallas_call(
        kernel,
        out_shape=(
            jax.ShapeDtypeStruct((rows, columns), bf16),
            jax.ShapeDtypeStruct((drows, columns), bf16),
        ),
        in_specs=[vmem] * 6,
        out_specs=(vmem, vmem),
        scratch_shapes=[
            pltpu.VMEM((2, rows, columns), bf16),
            pltpu.VMEM((RING, 2, rows, columns), bf16),
            pltpu.VMEM((RING, 2, rows, columns), bf16),
            pltpu.VMEM((RING, 2, drows, columns), bf16),
            pltpu.VMEM((2, rows, columns), bf16),
            pltpu.VMEM((2, rows, columns), bf16),
            pltpu.VMEM((2 * heads, rows, 1), f32),
            pltpu.VMEM((2 * heads, rows, 1), f32),
            pltpu.VMEM((2 * heads, rows, HEAD_DIM), f32),
            pltpu.VMEM((256, 128), f32),
            pltpu.VMEM((128, 128), f32),
            pltpu.VMEM((rows, columns), bf16),
            pltpu.VMEM((2, 8, 128), f32),
            pltpu.VMEM((rows, columns), bf16),
            pltpu.VMEM((2, 8, 128), f32),
            pltpu.VMEM((RING, 2 * drows, columns), bf16),
            pltpu.VMEM((RING, 8, 128), f32),
            pltpu.VMEM((RING, 2 * drows, columns), bf16),
            pltpu.VMEM((RING, 8, 128), f32),
            pltpu.VMEM((128, 128), f32),
            pltpu.VMEM((drows, columns), bf16),
            pltpu.VMEM((8, 128), f32),
            pltpu.VMEM((drows, columns), bf16),
            pltpu.VMEM((8, 128), f32),
            pltpu.VMEM((2 * drows, columns), f32),
        ]
        + [eight] * 16
        + [pltpu.SemaphoreType.DMA],
        compiler_params=pltpu.CompilerParams(
            collective_id=0, has_side_effects=True, vmem_limit_bytes=40 << 20
        ),
    )(query, key, value, dec_query, cross_key, cross_value)


def shards(enc_query, enc_key, enc_value, dec_query, cross_key, cross_value):
    arrays = (enc_key, enc_value, enc_query, cross_key, cross_value, dec_query)
    packed = jnp.concatenate(arrays, axis=0)
    count, columns = packed.shape
    tp = lax.axis_size("tp")
    packed = packed.reshape(count, tp, columns // tp).transpose(1, 0, 2)
    packed = lax.all_to_all(packed, "tp", split_axis=0, concat_axis=0, tiled=True)
    pieces, start = [], 0
    for array in arrays:
        piece = packed[:, start : start + array.shape[0]]
        pieces.append(piece.reshape(tp * array.shape[0], columns // tp))
        start += array.shape[0]
    key, value, query, ckey, cvalue, dquery = pieces
    return attention(query, key, value, dquery, ckey, cvalue)


def solution(mesh):
    in_specs = (P(("ctx", "tp"), None),) * 6
    out_specs = (P("ctx", "tp"), P("ctx", "tp"))
    return jax.shard_map(shards, mesh=mesh, in_specs=in_specs, out_specs=out_specs, check_vma=False)
```

time: 713 us -> 104 us (0.15)
  the two profiles are of different devices: /device:TPU:1 before, /device:TPU:5 now
where the time goes in v2:
time: 104 us; the launch traced here: 103 us
  Pallas kernels  62.5 us (60%)
  blocking collectives  26.9 us (26%)
  local copies, waits for them, and re-layouts  13 us (12%)
    pallas_call x1, Pallas kernels, attention(): pl.pallas_call(kernel, out_shape=(jax.ShapeDtypeStruct((rows, columns), b...  62.5 us
    all_to_all x1, blocking collectives, shards(): lax.all_to_all(packed, 'tp', split_axis=0, concat_axis=0, tiled=True)  26.9 us
    concatenate x1, local copies, waits for them, and re-layouts, shards(): packed = jnp.concatenate(arrays, axis=0)  11 us

profile of v2, /device:TPU:5, one launch (start us, length us, event | category | flops | bytes accessed | tf_op | source)
XLA Modules:
  0.0 103.1 jit_solution(14864612600294998918)
XLA Ops:
  0.6 11.0 %concatenate.3 = bf16[52,6144]{1,0:T(8,128)(2,1)S(1)} concatenate(bf16[10,6144]{1,0:T(8,128)(2,1)} %param.7, bf16[10,6144]{1,0:T(8,128)(2,1)} %param.8, bf16[10,6144]{1,0:T(8,128)(2,1)} %param.6, bf16[10,6144]{1,0:T(8,128)(2,1)} %param.10, bf16[10,6144]{1,0:T(8,128)(2,1)} %param.11, bf16[2,6144]{1,0:T(2,128)(2,1)} %param.9), dimensions={0} | concatenate | bytes 1277952 | tf_op jit(solution)/shard_map/concatenate | solution.py:325
  11.7 0.1 copy.10
  11.8 0.1 slice.30
  11.8 0.1 copy.12
  12.0 26.9 %all_to_all.5 = bf16[16,52,384]{2,1,0:T(8,128)(2,1)S(1)} all-to-all(bf16[16,52,384]{2,1,0:T(8,128)(2,1)S(1)} %bitcast.7), channel_id=1, replica_groups=mesh['ctx'=32,'tp'=16] {'tp'}, dimensions={0} | all-to-all | bytes 1277952 | tf_op jit(solution)/shard_map/all_to_all | solution.py:329
  38.9 0.2 fusion
  39.1 0.1 reshape.31.cv_ref
  39.1 0.1 reshape.30.ck_ref
  39.2 0.1 reshape.28.v_ref
  39.2 0.1 reshape.27.k_ref
  39.3 0.1 reshape.26.q_ref
  39.4 62.5 %shard_map.77 = (bf16[160,384]{1,0:T(8,128)(2,1)S(1)}, bf16[32,384]{1,0:T(8,128)(2,1)S(1)}) custom-call(bf16[160,384]{1,0:T(8,128)(2,1)S(1)} %reshape.26.q_ref, bf16[160,384]{1,0:T(8,128)(2,1)S(1)} %reshape.27.k_ref, bf16[160,384]{1,0:T(8,128)(2,1)S(1)} %reshape.28.v_ref, bf16[32,384]{1,0:T(8,128)(2,1)S(1)} %reshape.29.dq_ref, ...), custom_call_target="tpu_custom_call" | custom-call | tf_op jit(solution)/shard_map/pallas_call | solution.py:280
  101.8 0.7 copy.15
  102.5 0.6 copy.16
  (2 shorter events, 0.0 us)

commit v3 on v2

--- a/solution.py
+++ b/solution.py
@@ -21,14 +21,19 @@
 
 
 def kernel(
-    q_ref, k_ref, v_ref, dq_ref, ck_ref, cv_ref, enc_ref, dec_ref,
-    qb, kb, vb, db, ckb, cvb, top, total, acc, estat, dstat,
+    q_arg, k_arg, v_arg, dq_arg, ck_arg, cv_arg, enc_ref, dec_ref,
+    q_parts, k_parts, v_parts, dq_parts, ck_parts, cv_parts,
+    dq_ref, qb, kb, vb, db, ckb, cvb, top, total, acc, estat, dstat,
     esend, esend_stat, eback, eback_stat, psend, psend_stat, pback, pback_stat,
     wide, zsend, zsend_stat, zback, zback_stat, dmix,
-    ks, kr, vs, vr, ds, dr, kps, kpr, vps, vpr, rs, rr, rts, rtr, ms, mr, local,
+    ks, kr, vs, vr, ds, dr, kps, kpr, vps, vpr, rs, rr, rts, rtr, ms, mr, ts, tr, self_sems,
 ):
-    rows, columns = q_ref.shape
+    rows, columns = enc_ref.shape
     drows = dq_ref.shape[0]
+    tokens = q_arg.shape[0]
+    dtokens = dq_arg.shape[0]
+    group = q_parts.shape[0]
+    here = lax.axis_index("tp")
     heads = columns // HEAD_DIM
     me = lax.axis_index("ctx")
     plane, y, core = me // (2 * RING), (me // 2) % RING, me % 2
@@ -42,7 +47,11 @@
     barrier = pltpu.get_barrier_semaphore()
     for peer in [along(offset) for offset in range(1, RING)] + [twin, mirror]:
         pl.semaphore_signal(barrier, inc=1, device_id=peer, device_id_type=MESH)
-    pl.semaphore_wait(barrier, RING + 1)
+    for offset in range(1, group):
+        pl.semaphore_signal(
+            barrier, inc=1, device_id={"tp": lax.rem(here + offset, group)}, device_id_type=MESH
+        )
+    pl.semaphore_wait(barrier, RING + group)
 
     started = []
 
@@ -85,24 +94,81 @@
     def query_slot(slot):
         return db.at[slot]
 
+    exchanges = (
+        (dq_arg, dq_parts), (k_arg, k_parts), (v_arg, v_parts),
+        (q_arg, q_parts), (ck_arg, ck_parts), (cv_arg, cv_parts),
+    )
+
+    def slab(which, peer):
+        argument, parts = exchanges[which]
+        return argument.at[:, pl.ds(pl.multiple_of(peer * columns, 128), columns)]
+
+    def slab_copy(which, offset):
+        peer = lax.rem(here + offset, group)
+        return pltpu.make_async_remote_copy(
+            src_ref=slab(which, peer), dst_ref=exchanges[which][1].at[here],
+            send_sem=ts.at[which, offset], recv_sem=tr.at[which, here],
+            device_id={"tp": peer}, device_id_type=MESH,
+        )
+
+    def self_copy(which):
+        return pltpu.make_async_copy(slab(which, here), exchanges[which][1].at[here], self_sems.at[which])
+
+    for which in range(6):
+        self_copy(which).start()
+
+        def start_one(offset, carry):
+            slab_copy(which, offset).start()
+            return carry
+
+        lax.fori_loop(1, group, start_one, 0)
+
+    def gather(which):
+        parts = exchanges[which][1]
+
+        def wait_one(offset, carry):
+            origin = lax.rem(here + offset, group)
+            pltpu.make_async_remote_copy(
+                src_ref=parts.at[origin], dst_ref=parts.at[origin],
+                send_sem=ts.at[which, offset], recv_sem=tr.at[which, origin],
+                device_id=twin, device_id_type=MESH,
+            ).wait_recv()
+            return carry
+
+        lax.fori_loop(1, group, wait_one, 0)
+        self_copy(which).wait()
+        return parts
+
+    parts = gather(0)
+    for source in range(group):
+        piece = parts[source]
+        dq_ref[source * dtokens : (source + 1) * dtokens, :] = piece
+        db[0, 0, source * dtokens : (source + 1) * dtokens, :] = piece
     send(dq_ref, db.at[0, 1], ms.at[0], mr.at[0], mirror)
-    pass_on(k_ref, 0, key_slot, ks, kr, KEY_RIGHT)
-    pass_on(v_ref, 0, value_slot, vs, vr, VALUE_RIGHT)
-    send(k_ref, kb.at[0, 1], kps.at[0], kpr.at[0], twin)
-    send(v_ref, vb.at[0, 1], vps.at[0], vpr.at[0], twin)
-    send(q_ref, qb.at[1], ms.at[1], mr.at[1], mirror)
-    send(ck_ref, ckb.at[1], ms.at[2], mr.at[2], twin)
-    send(cv_ref, cvb.at[1], ms.at[3], mr.at[3], twin)
-    own = pltpu.make_async_copy(dq_ref, db.at[0, 0], local)
-    own.start()
-    kb[0, 0] = k_ref[...]
-    vb[0, 0] = v_ref[...]
-    qb[0] = q_ref[...]
-    ckb[0] = ck_ref[...]
-    cvb[0] = cv_ref[...]
-    own.wait()
+    parts = gather(1)
+    for source in range(group):
+        kb[0, 0, source * tokens : (source + 1) * tokens, :] = parts[source]
+    pass_on(kb.at[0, 0], 0, key_slot, ks, kr, KEY_RIGHT)
+    send(kb.at[0, 0], kb.at[0, 1], kps.at[0], kpr.at[0], twin)
+    parts = gather(2)
+    for source in range(group):
+        vb[0, 0, source * tokens : (source + 1) * tokens, :] = parts[source]
+    pass_on(vb.at[0, 0], 0, value_slot, vs, vr, VALUE_RIGHT)
+    send(vb.at[0, 0], vb.at[0, 1], vps.at[0], vpr.at[0], twin)
     arrived(db.at[0, 1], mr.at[0])
     pass_on(db.at[0], 0, query_slot, ds, dr, KEY_RIGHT)
+    parts = gather(3)
+    for source in range(group):
+        qb[0, source * tokens : (source + 1) * tokens, :] = parts[source]
+    send(qb.at[0], qb.at[1], ms.at[1], mr.at[1], mirror)
+    parts = gather(4)
+    for source in range(group):
+        ckb[0, source * tokens : (source + 1) * tokens, :] = parts[source]
+    send(ckb.at[0], ckb.at[1], ms.at[2], mr.at[2], twin)
+    parts = gather(5)
+    for source in range(group):
+        cvb[0, source * tokens : (source + 1) * tokens, :] = parts[source]
+    send(cvb.at[0], cvb.at[1], ms.at[3], mr.at[3], twin)
     estat[...] = jnp.zeros_like(estat)
     dstat[...] = jnp.zeros_like(dstat)
     wide[...] = jnp.zeros_like(wide)
@@ -268,11 +334,19 @@
 
     for copy in started:
         copy.wait_send()
+    for which in range(6):
+
+        def drain_one(offset, carry):
+            slab_copy(which, offset).wait_send()
+            return carry
+
+        lax.fori_loop(1, group, drain_one, 0)
 
 
 def attention(query, key, value, dec_query, cross_key, cross_value):
-    rows, columns = query.shape
-    drows = dec_query.shape[0]
+    group = lax.axis_size("tp")
+    tokens, dtokens = query.shape[0], dec_query.shape[0]
+    rows, drows, columns = group * tokens, group * dtokens, query.shape[1] // group
     heads = columns // HEAD_DIM
     bf16, f32 = jnp.bfloat16, jnp.float32
     vmem = pl.BlockSpec(memory_space=pltpu.VMEM)
@@ -283,9 +357,16 @@
             jax.ShapeDtypeStruct((rows, columns), bf16),
             jax.ShapeDtypeStruct((drows, columns), bf16),
         ),
-        in_specs=[vmem] * 6,
+        in_specs=[pl.BlockSpec(memory_space=pl.ANY)] * 6,
         out_specs=(vmem, vmem),
         scratch_shapes=[
+            pltpu.VMEM((group, tokens, columns), bf16),
+            pltpu.VMEM((group, tokens, columns), bf16),
+            pltpu.VMEM((group, tokens, columns), bf16),
+            pltpu.VMEM((group, dtokens, columns), bf16),
+            pltpu.VMEM((group, tokens, columns), bf16),
+            pltpu.VMEM((group, tokens, columns), bf16),
+            pltpu.VMEM((drows, columns), bf16),
             pltpu.VMEM((2, rows, columns), bf16),
             pltpu.VMEM((RING, 2, rows, columns), bf16),
             pltpu.VMEM((RING, 2, rows, columns), bf16),
@@ -313,7 +394,8 @@
             pltpu.VMEM((2 * drows, columns), f32),
         ]
         + [eight] * 16
-        + [pltpu.SemaphoreType.DMA],
+        + [pltpu.SemaphoreType.DMA((6, group))] * 2
+        + [pltpu.SemaphoreType.DMA((6,))],
         compiler_params=pltpu.CompilerParams(
             collective_id=0, has_side_effects=True, vmem_limit_bytes=40 << 20
         ),
@@ -321,19 +403,7 @@
 
 
 def shards(enc_query, enc_key, enc_value, dec_query, cross_key, cross_value):
-    arrays = (enc_key, enc_value, enc_query, cross_key, cross_value, dec_query)
-    packed = jnp.concatenate(arrays, axis=0)
-    count, columns = packed.shape
-    tp = lax.axis_size("tp")
-    packed = packed.reshape(count, tp, columns // tp).transpose(1, 0, 2)
-    packed = lax.all_to_all(packed, "tp", split_axis=0, concat_axis=0, tiled=True)
-    pieces, start = [], 0
-    for array in arrays:
-        piece = packed[:, start : start + array.shape[0]]
-        pieces.append(piece.reshape(tp * array.shape[0], columns // tp))
-        start += array.shape[0]
-    key, value, query, ckey, cvalue, dquery = pieces
-    return attention(query, key, value, dquery, ckey, cvalue)
+    return attention(enc_query, enc_key, enc_value, dec_query, cross_key, cross_value)
 
 
 def solution(mesh):

time: 104 us -> 96 us (0.923)
  the two profiles are of different devices: /device:TPU:5 before, /device:TPU:8 now
where the time goes in v3:
time: 96 us; the launch traced here: 95.7 us
  Pallas kernels  88.4 us (92%)
  local copies, waits for them, and re-layouts  6.62 us (7%)
    pallas_call x1, Pallas kernels, attention(): pl.pallas_call(kernel, out_shape=(jax.ShapeDtypeStruct((rows, columns), b...  88.4 us
    unnamed x14, local copies, waits for them, and re-layouts  6.62 us

profile of v3, /device:TPU:8, one launch (start us, length us, event | category | flops | bytes accessed | tf_op | source)
XLA Modules:
  0.0 95.7 jit_solution(2864414609131474076)
XLA Ops:
  0.6 0.0 copy-start
  0.6 0.9 copy-done
  1.6 0.0 copy-start.1
  1.6 0.9 copy-done.1
  2.5 0.0 copy-start.2
  2.5 0.9 copy-done.2
  3.4 0.0 copy-start.3
  3.4 0.9 copy-done.3
  4.3 0.0 copy-start.4
  4.3 0.9 copy-done.4
  5.3 0.0 copy-start.5
  5.3 0.7 copy-done.5
  6.0 88.4 %shard_map.77 = (bf16[160,384]{1,0:T(8,128)(2,1)S(1)}, bf16[32,384]{1,0:T(8,128)(2,1)S(1)}) custom-call(bf16[10,6144]{1,0:T(8,128)(2,1)S(1)} %copy-done, bf16[10,6144]{1,0:T(8,128)(2,1)S(1)} %copy-done.1, bf16[10,6144]{1,0:T(8,128)(2,1)S(1)} %copy-done.2, bf16[2,6144]{1,0:T(2,128)(2,1)S(1)} %copy-done.5, bf16[10,6144]{1,0:T(8,128)(2,1)S(1)} %copy-done.3, ...), custom_call_target="tpu_custom_call" | custom-call | tf_op jit(solution)/shard_map/pallas_call | solution.py:354
  94.4 0.7 copy.10
  95.1 0.6 copy.11
Async XLA Ops:
  0.6 0.9 copy-start
  1.6 0.9 copy-start.1
  2.5 0.9 copy-start.2
  3.4 0.9 copy-start.3
  4.3 0.9 copy-start.4
  5.3 0.7 copy-start.5

commit v4 on v3

--- a/solution.py
+++ b/solution.py
@@ -139,43 +139,13 @@
         self_copy(which).wait()
         return parts
 
-    parts = gather(0)
-    for source in range(group):
-        piece = parts[source]
-        dq_ref[source * dtokens : (source + 1) * dtokens, :] = piece
-        db[0, 0, source * dtokens : (source + 1) * dtokens, :] = piece
-    send(dq_ref, db.at[0, 1], ms.at[0], mr.at[0], mirror)
-    parts = gather(1)
-    for source in range(group):
-        kb[0, 0, source * tokens : (source + 1) * tokens, :] = parts[source]
-    pass_on(kb.at[0, 0], 0, key_slot, ks, kr, KEY_RIGHT)
-    send(kb.at[0, 0], kb.at[0, 1], kps.at[0], kpr.at[0], twin)
-    parts = gather(2)
-    for source in range(group):
-        vb[0, 0, source * tokens : (source + 1) * tokens, :] = parts[source]
-    pass_on(vb.at[0, 0], 0, value_slot, vs, vr, VALUE_RIGHT)
-    send(vb.at[0, 0], vb.at[0, 1], vps.at[0], vpr.at[0], twin)
-    arrived(db.at[0, 1], mr.at[0])
-    pass_on(db.at[0], 0, query_slot, ds, dr, KEY_RIGHT)
-    parts = gather(3)
-    for source in range(group):
-        qb[0, source * tokens : (source + 1) * tokens, :] = parts[source]
-    send(qb.at[0], qb.at[1], ms.at[1], mr.at[1], mirror)
-    parts = gather(4)
-    for source in range(group):
-        ckb[0, source * tokens : (source + 1) * tokens, :] = parts[source]
-    send(ckb.at[0], ckb.at[1], ms.at[2], mr.at[2], twin)
-    parts = gather(5)
-    for source in range(group):
-        cvb[0, source * tokens : (source + 1) * tokens, :] = parts[source]
-    send(cvb.at[0], cvb.at[1], ms.at[3], mr.at[3], twin)
     estat[...] = jnp.zeros_like(estat)
     dstat[...] = jnp.zeros_like(dstat)
     wide[...] = jnp.zeros_like(wide)
 
-    def attend(slots, first):
-        def body(item, carry):
-            half, head = item // heads, item % heads
+    def attend(half, slots, first=False):
+        def body(head, carry):
+            item = half * heads + head
             at = pl.ds(pl.multiple_of(head * HEAD_DIM, HEAD_DIM), HEAD_DIM)
             query = qb[half, :, at]
             parts = [scores_of(query, kb[slot, :, :, at].reshape(2 * rows, HEAD_DIM)) for slot in slots]
@@ -202,7 +172,7 @@
             acc[item] = mixed
             return carry
 
-        lax.fori_loop(0, 2 * heads, body, 0)
+        lax.fori_loop(0, heads, body, 0)
 
     def visit(slot):
         def body(head, carry):
@@ -232,15 +202,14 @@
             pback[0] = psend[0]
             pback_stat[0] = psend_stat[0]
 
-    arrived(kb.at[0, 1], kpr.at[0])
-    arrived(vb.at[0, 1], vpr.at[0])
-    arrived(qb.at[1], mr.at[1])
-    attend((0,), True)
-    arrived(ckb.at[1], mr.at[2])
-    arrived(cvb.at[1], mr.at[3])
-    visit(0)
-
-    for step in range(1, RING // 2 + 1):
+    def place(which, *targets):
+        parts = gather(which)
+        count = parts.shape[1]
+        for source in range(group):
+            for target in targets:
+                target[source * count : (source + 1) * count, :] = parts[source]
+
+    def hop(step):
         pair = (step,) if step == RING - step else (step, RING - step)
         for slot in pair:
             arrived(kb.at[slot, 0], kr.at[slot])
@@ -250,15 +219,59 @@
             arrived(vb.at[slot, 0], vr.at[slot])
             pass_on(vb.at[slot, 0], slot, value_slot, vs, vr, VALUE_RIGHT)
             send(vb.at[slot, 0], vb.at[slot, 1], vps.at[slot], vpr.at[slot], twin)
-        for slot in pair:
+
+    def query_hop(step):
+        for slot in (step,) if step == RING - step else (step, RING - step):
             arrived(db.at[slot], dr.at[slot])
             pass_on(db.at[slot], slot, query_slot, ds, dr, KEY_RIGHT)
-        for slot in pair:
-            visit(slot)
-        for slot in pair:
+
+    def from_twin(*slots):
+        for slot in slots:
             arrived(kb.at[slot, 1], kpr.at[slot])
             arrived(vb.at[slot, 1], vpr.at[slot])
-        attend(pair, False)
+
+    place(0, dq_ref, db.at[0, 0])
+    send(dq_ref, db.at[0, 1], ms.at[0], mr.at[0], mirror)
+    place(1, kb.at[0, 0])
+    pass_on(kb.at[0, 0], 0, key_slot, ks, kr, KEY_RIGHT)
+    send(kb.at[0, 0], kb.at[0, 1], kps.at[0], kpr.at[0], twin)
+    arrived(db.at[0, 1], mr.at[0])
+    pass_on(db.at[0], 0, query_slot, ds, dr, KEY_RIGHT)
+    place(2, vb.at[0, 0])
+    pass_on(vb.at[0, 0], 0, value_slot, vs, vr, VALUE_RIGHT)
+    send(vb.at[0, 0], vb.at[0, 1], vps.at[0], vpr.at[0], twin)
+    query_hop(1)
+    hop(1)
+    query_hop(2)
+    place(3, qb.at[0])
+    send(qb.at[0], qb.at[1], ms.at[1], mr.at[1], mirror)
+    from_twin(0)
+    attend(0, (0,), True)
+    hop(2)
+    query_hop(3)
+    from_twin(1, 7)
+    attend(0, (1, 7))
+    place(4, ckb.at[0])
+    send(ckb.at[0], ckb.at[1], ms.at[2], mr.at[2], twin)
+    place(5, cvb.at[0])
+    send(cvb.at[0], cvb.at[1], ms.at[3], mr.at[3], twin)
+    hop(3)
+    query_hop(4)
+    from_twin(2, 6)
+    attend(0, (2, 6))
+    arrived(ckb.at[1], mr.at[2])
+    arrived(cvb.at[1], mr.at[3])
+    for slot in (4, 3, 5, 2, 6, 1, 7, 0):
+        visit(slot)
+    arrived(qb.at[1], mr.at[1])
+    attend(1, (0,), True)
+    attend(1, (1, 7))
+    attend(1, (2, 6))
+    from_twin(3, 5)
+    attend(1, (3, 5))
+    hop(4)
+    from_twin(4)
+    attend(1, (4,))
 
     lane = lax.broadcasted_iota(jnp.int32, (rows, HEAD_DIM), 1)
     held = jnp.zeros((rows, HEAD_DIM), jnp.float32)
@@ -272,6 +285,8 @@
         esend_stat[chunk] = jnp.transpose(estat[chunk * 128 : (chunk + 1) * 128, :])[0:8]
     send(esend, eback, ms.at[4], mr.at[4], mirror)
     send(esend_stat, eback_stat, ms.at[5], mr.at[5], mirror)
+    attend(0, (3, 5))
+    attend(0, (4,))
 
     for slot in range(1, RING):
         arrived(pback.at[slot], rr.at[slot])
@@ -397,7 +412,7 @@
         + [pltpu.SemaphoreType.DMA((6, group))] * 2
         + [pltpu.SemaphoreType.DMA((6,))],
         compiler_params=pltpu.CompilerParams(
-            collective_id=0, has_side_effects=True, vmem_limit_bytes=40 << 20
+            collective_id=0, has_side_effects=True, vmem_limit_bytes=67043328
         ),
     )(query, key, value, dec_query, cross_key, cross_value)
 

time: 96 us -> 90.5 us (0.943)
  the two profiles are of different devices: /device:TPU:8 before, /device:TPU:1 now
where the time goes in v4:
time: 90.5 us; the launch traced here: 90.4 us
  Pallas kernels  87.5 us (97%)
  local copies, waits for them, and re-layouts  2.18 us (2%)
    pallas_call x1, Pallas kernels, attention(): pl.pallas_call(kernel, out_shape=(jax.ShapeDtypeStruct((rows, columns), b...  87.5 us
    unnamed x4, local copies, waits for them, and re-layouts  2.18 us

profile of v4, /device:TPU:1, one launch (start us, length us, event | category | flops | bytes accessed | tf_op | source)
XLA Modules:
  0.0 90.4 jit_solution(1120843833629920730)
XLA Ops:
  0.6 87.5 %shard_map.77 = (bf16[160,384]{1,0:T(8,128)(2,1)}, bf16[32,384]{1,0:T(8,128)(2,1)}) custom-call(bf16[10,6144]{1,0:T(8,128)(2,1)} %q_arg.1, bf16[10,6144]{1,0:T(8,128)(2,1)} %k_arg.1, bf16[10,6144]{1,0:T(8,128)(2,1)} %v_arg.1, bf16[2,6144]{1,0:T(2,128)(2,1)} %dq_arg.1, bf16[10,6144]{1,0:T(8,128)(2,1)} %ck_arg.1, bf16[10,6144]{1,0:T(8,128)(2,1)} %cv_arg.1), custom_call_target="tpu_custom_call" | custom-call | tf_op jit(solution)/shard_map/pallas_call | solution.py:369
  88.2 0.0 copy-start
  88.2 1.6 %copy.10 = bf16[160,384]{1,0:T(8,128)(2,1)} copy(bf16[160,384]{1,0:T(8,128)(2,1)} %get-tuple-element.4) | data formatting | bytes 245760
  89.8 0.0 copy-done
  89.8 0.6 copy.11
Async XLA Ops:
  88.2 1.6 %copy-start = (bf16[32,384]{1,0:T(8,128)(2,1)S(1)}, bf16[32,384]{1,0:T(8,128)(2,1)}, u32[]{:S(2)}) copy-start(bf16[32,384]{1,0:T(8,128)(2,1)} %get-tuple-element.5) | copy-start | bytes 73732

commit v5 on v4

--- a/solution.py
+++ b/solution.py
@@ -143,15 +143,16 @@
     dstat[...] = jnp.zeros_like(dstat)
     wide[...] = jnp.zeros_like(wide)
 
-    def attend(half, slots, first=False):
+    def attend(span, slots, first=False):
+        count = span.stop - span.start
+
         def body(head, carry):
-            item = half * heads + head
             at = pl.ds(pl.multiple_of(head * HEAD_DIM, HEAD_DIM), HEAD_DIM)
-            query = qb[half, :, at]
+            query = qb[:, :, at].reshape(2 * rows, HEAD_DIM)[span]
             parts = [scores_of(query, kb[slot, :, :, at].reshape(2 * rows, HEAD_DIM)) for slot in slots]
             new_top = functools.reduce(jnp.maximum, [jnp.max(part, axis=1, keepdims=True) for part in parts])
             if not first:
-                new_top = jnp.maximum(new_top, top[item])
+                new_top = jnp.maximum(new_top, top[head, span])
             mixed, summed = None, None
             for slot, part in zip(slots, parts):
                 weights = jnp.exp2((part - new_top) * STEEP)
@@ -164,20 +165,25 @@
                 summed = one if summed is None else summed + one
                 mixed = two if mixed is None else mixed + two
             if not first:
-                shrink = jnp.exp2((top[item] - new_top) * STEEP)
-                summed = summed + total[item] * shrink
-                mixed = mixed + acc[item] * shrink
-            top[item] = new_top
-            total[item] = summed
-            acc[item] = mixed
+                shrink = jnp.exp2((top[head, span] - new_top) * STEEP)
+                summed = summed + total[head, span] * shrink
+                mixed = mixed + acc[head, span] * shrink
+            top[head, span] = new_top
+            total[head, span] = summed
+            acc[head, span] = mixed
             return carry
 
         lax.fori_loop(0, heads, body, 0)
 
-    def visit(slot):
-        def body(head, carry):
+    own_rows, mirror_rows, both = slice(0, rows), slice(rows, 2 * rows), slice(0, 2 * rows)
+
+    def visit_all():
+        some = RING // 2
+
+        def body(item, carry):
+            start, head = (item // heads) * some, item % heads
             at = pl.ds(pl.multiple_of(head * HEAD_DIM, HEAD_DIM), HEAD_DIM)
-            query = db[slot, :, :, at].reshape(2 * drows, HEAD_DIM)
+            query = db[pl.ds(start, some), :, :, at].reshape(some * 2 * drows, HEAD_DIM)
             part = scores_of(query, ckb[:, :, at].reshape(2 * rows, HEAD_DIM))
             row_top = jnp.max(part, axis=1, keepdims=True)
             weights = jnp.exp2((part - row_top) * STEEP)
@@ -186,21 +192,21 @@
                 weights.astype(jnp.bfloat16), cvb[:, :, at].reshape(2 * rows, HEAD_DIM),
                 preferred_element_type=jnp.float32,
             )
-            psend[slot, :, at] = mixed.astype(jnp.bfloat16)
-            lane = lax.broadcasted_iota(jnp.int32, (2 * drows, HEAD_DIM), 1)
-            held = dstat[0 : 2 * drows, :]
-            held = jnp.where(lane == head, row_top, held)
-            dstat[0 : 2 * drows, :] = jnp.where(lane == heads + head, summed, held)
+            psend[pl.ds(start, some), :, at] = mixed.astype(jnp.bfloat16).reshape(some, 2 * drows, HEAD_DIM)
+            lane = lax.broadcasted_iota(jnp.int32, (some, 2 * drows, HEAD_DIM), 2)
+            held = dstat[pl.ds(start, some), 0 : 2 * drows, :]
+            held = jnp.where(lane == head, row_top.reshape(some, 2 * drows, 1), held)
+            held = jnp.where(lane == heads + head, summed.reshape(some, 2 * drows, 1), held)
+            dstat[pl.ds(start, some), 0 : 2 * drows, :] = held
             return carry
 
-        lax.fori_loop(0, heads, body, 0)
-        psend_stat[slot] = jnp.transpose(dstat[...])[0:8]
-        if slot > 0:
+        lax.fori_loop(0, 2 * heads, body, 0)
+        for slot in (4, 3, 5, 2, 6, 1, 7):
+            psend_stat[slot] = jnp.transpose(dstat[slot])[0:8]
             send(psend.at[slot], pback.at[slot], rs.at[slot], rr.at[slot], along(-slot))
             send(psend_stat.at[slot], pback_stat.at[slot], rts.at[slot], rtr.at[slot], along(-slot))
-        else:
-            pback[0] = psend[0]
-            pback_stat[0] = psend_stat[0]
+        pback[0] = psend[0]
+        pback_stat[0] = jnp.transpose(dstat[0])[0:8]
 
     def place(which, *targets):
         parts = gather(which)
@@ -245,48 +251,42 @@
     query_hop(2)
     place(3, qb.at[0])
     send(qb.at[0], qb.at[1], ms.at[1], mr.at[1], mirror)
-    from_twin(0)
-    attend(0, (0,), True)
     hop(2)
     query_hop(3)
-    from_twin(1, 7)
-    attend(0, (1, 7))
     place(4, ckb.at[0])
     send(ckb.at[0], ckb.at[1], ms.at[2], mr.at[2], twin)
     place(5, cvb.at[0])
     send(cvb.at[0], cvb.at[1], ms.at[3], mr.at[3], twin)
     hop(3)
     query_hop(4)
-    from_twin(2, 6)
-    attend(0, (2, 6))
     arrived(ckb.at[1], mr.at[2])
     arrived(cvb.at[1], mr.at[3])
-    for slot in (4, 3, 5, 2, 6, 1, 7, 0):
-        visit(slot)
+    visit_all()
     arrived(qb.at[1], mr.at[1])
-    attend(1, (0,), True)
-    attend(1, (1, 7))
-    attend(1, (2, 6))
+    from_twin(0)
+    attend(both, (0,), True)
+    from_twin(1, 7)
+    attend(both, (1, 7))
+    from_twin(2, 6)
+    attend(both, (2, 6))
     from_twin(3, 5)
-    attend(1, (3, 5))
+    attend(both, (3, 5))
     hop(4)
     from_twin(4)
-    attend(1, (4,))
+    attend(mirror_rows, (4,))
 
     lane = lax.broadcasted_iota(jnp.int32, (rows, HEAD_DIM), 1)
     held = jnp.zeros((rows, HEAD_DIM), jnp.float32)
     for head in range(heads):
-        item = heads + head
-        esend[:, head * HEAD_DIM : (head + 1) * HEAD_DIM] = acc[item].astype(jnp.bfloat16)
-        held = jnp.where(lane == head, top[item], held)
-        held = jnp.where(lane == heads + head, total[item], held)
+        esend[:, head * HEAD_DIM : (head + 1) * HEAD_DIM] = acc[head, mirror_rows].astype(jnp.bfloat16)
+        held = jnp.where(lane == head, top[head, mirror_rows], held)
+        held = jnp.where(lane == heads + head, total[head, mirror_rows], held)
     estat[0:rows, :] = held
     for chunk in range(2):
         esend_stat[chunk] = jnp.transpose(estat[chunk * 128 : (chunk + 1) * 128, :])[0:8]
     send(esend, eback, ms.at[4], mr.at[4], mirror)
     send(esend_stat, eback_stat, ms.at[5], mr.at[5], mirror)
-    attend(0, (3, 5))
-    attend(0, (4,))
+    attend(own_rows, (4,))
 
     for slot in range(1, RING):
         arrived(pback.at[slot], rr.at[slot])
@@ -324,11 +324,11 @@
         span = slice(head * HEAD_DIM, (head + 1) * HEAD_DIM)
         other_top = estat[0:rows, head : head + 1]
         other_total = estat[0:rows, heads + head : heads + head + 1]
-        peak = jnp.maximum(top[head], other_top)
-        mine = jnp.exp2((top[head] - peak) * STEEP)
+        peak = jnp.maximum(top[head, own_rows], other_top)
+        mine = jnp.exp2((top[head, own_rows] - peak) * STEEP)
         theirs = jnp.exp2((other_top - peak) * STEEP)
-        whole = mine * acc[head] + theirs * eback[:, span].astype(jnp.float32)
-        enc_ref[:, span] = (whole / (mine * total[head] + theirs * other_total)).astype(jnp.bfloat16)
+        whole = mine * acc[head, own_rows] + theirs * eback[:, span].astype(jnp.float32)
+        enc_ref[:, span] = (whole / (mine * total[head, own_rows] + theirs * other_total)).astype(jnp.bfloat16)
 
     arrived(zback, mr.at[6])
     arrived(zback_stat, mr.at[7])
@@ -388,11 +388,11 @@
             pltpu.VMEM((RING, 2, drows, columns), bf16),
             pltpu.VMEM((2, rows, columns), bf16),
             pltpu.VMEM((2, rows, columns), bf16),
-            pltpu.VMEM((2 * heads, rows, 1), f32),
-            pltpu.VMEM((2 * heads, rows, 1), f32),
-            pltpu.VMEM((2 * heads, rows, HEAD_DIM), f32),
+            pltpu.VMEM((heads, 2 * rows, 1), f32),
+            pltpu.VMEM((heads, 2 * rows, 1), f32),
+            pltpu.VMEM((heads, 2 * rows, HEAD_DIM), f32),
             pltpu.VMEM((256, 128), f32),
-            pltpu.VMEM((128, 128), f32),
+            pltpu.VMEM((RING, 128, 128), f32),
             pltpu.VMEM((rows, columns), bf16),
             pltpu.VMEM((2, 8, 128), f32),
             pltpu.VMEM((rows, columns), bf16),

time: 90.5 us -> 82.6 us (0.913)
  Pallas kernels: 87.5 us -> 79.6 us
    pallas_call x1, Pallas kernels: 87.5 us -> 79.6 us  [attention(): pl.pallas_call(kernel, out_shape=(jax.ShapeDtypeStruct((rows, columns), b...]
where the time goes in v5:
time: 82.6 us; the launch traced here: 82.5 us
  Pallas kernels  79.6 us (96%)
  local copies, waits for them, and re-layouts  2.18 us (3%)
    pallas_call x1, Pallas kernels, attention(): pl.pallas_call(kernel, out_shape=(jax.ShapeDtypeStruct((rows, columns), b...  79.6 us
    unnamed x4, local copies, waits for them, and re-layouts  2.18 us

profile of v5, /device:TPU:1, one launch (start us, length us, event | category | flops | bytes accessed | tf_op | source)
XLA Modules:
  0.0 82.5 jit_solution(12430010190167461670)
XLA Ops:
  0.6 79.6 %shard_map.77 = (bf16[160,384]{1,0:T(8,128)(2,1)}, bf16[32,384]{1,0:T(8,128)(2,1)}) custom-call(bf16[10,6144]{1,0:T(8,128)(2,1)} %q_arg.1, bf16[10,6144]{1,0:T(8,128)(2,1)} %k_arg.1, bf16[10,6144]{1,0:T(8,128)(2,1)} %v_arg.1, bf16[2,6144]{1,0:T(2,128)(2,1)} %dq_arg.1, bf16[10,6144]{1,0:T(8,128)(2,1)} %ck_arg.1, bf16[10,6144]{1,0:T(8,128)(2,1)} %cv_arg.1), custom_call_target="tpu_custom_call" | custom-call | tf_op jit(solution)/shard_map/pallas_call | solution.py:369
  80.3 0.0 copy-start
  80.3 1.6 %copy.10 = bf16[160,384]{1,0:T(8,128)(2,1)} copy(bf16[160,384]{1,0:T(8,128)(2,1)} %get-tuple-element.4) | data formatting | bytes 245760
  81.8 0.0 copy-done
  81.8 0.6 copy.11
Async XLA Ops:
  80.3 1.6 %copy-start = (bf16[32,384]{1,0:T(8,128)(2,1)S(1)}, bf16[32,384]{1,0:T(8,128)(2,1)}, u32[]{:S(2)}) copy-start(bf16[32,384]{1,0:T(8,128)(2,1)} %get-tuple-element.5) | copy-start | bytes 73732

commit v6 on v5

--- a/solution.py
+++ b/solution.py
@@ -201,12 +201,15 @@
             return carry
 
         lax.fori_loop(0, 2 * heads, body, 0)
+        for slot in range(1, RING):
+            psend_stat[slot] = jnp.transpose(dstat[slot])[0:8]
+        pback[0] = psend[0]
+        pback_stat[0] = jnp.transpose(dstat[0])[0:8]
+
+    def give_back():
         for slot in (4, 3, 5, 2, 6, 1, 7):
-            psend_stat[slot] = jnp.transpose(dstat[slot])[0:8]
             send(psend.at[slot], pback.at[slot], rs.at[slot], rr.at[slot], along(-slot))
             send(psend_stat.at[slot], pback_stat.at[slot], rts.at[slot], rtr.at[slot], along(-slot))
-        pback[0] = psend[0]
-        pback_stat[0] = jnp.transpose(dstat[0])[0:8]
 
     def place(which, *targets):
         parts = gather(which)
@@ -272,6 +275,7 @@
     from_twin(3, 5)
     attend(both, (3, 5))
     hop(4)
+    give_back()
     from_twin(4)
     attend(mirror_rows, (4,))
 

time: 82.6 us -> 85.1 us (1.030)
  the two profiles are of different devices: /device:TPU:1 before, /device:TPU:6 now
where the time goes in v6:
time: 85.1 us; the launch traced here: 85 us
  Pallas kernels  82.1 us (96%)
  local copies, waits for them, and re-layouts  2.18 us (3%)
    pallas_call x1, Pallas kernels, attention(): pl.pallas_call(kernel, out_shape=(jax.ShapeDtypeStruct((rows, columns), b...  82.1 us
    unnamed x4, local copies, waits for them, and re-layouts  2.18 us

profile of v6, /device:TPU:6, one launch (start us, length us, event | category | flops | bytes accessed | tf_op | source)
XLA Modules:
  0.0 85.0 jit_solution(878615936653549459)
XLA Ops:
  0.6 82.1 %shard_map.77 = (bf16[160,384]{1,0:T(8,128)(2,1)}, bf16[32,384]{1,0:T(8,128)(2,1)}) custom-call(bf16[10,6144]{1,0:T(8,128)(2,1)} %q_arg.1, bf16[10,6144]{1,0:T(8,128)(2,1)} %k_arg.1, bf16[10,6144]{1,0:T(8,128)(2,1)} %v_arg.1, bf16[2,6144]{1,0:T(2,128)(2,1)} %dq_arg.1, bf16[10,6144]{1,0:T(8,128)(2,1)} %ck_arg.1, bf16[10,6144]{1,0:T(8,128)(2,1)} %cv_arg.1), custom_call_target="tpu_custom_call" | custom-call | tf_op jit(solution)/shard_map/pallas_call | solution.py:373
  82.8 0.0 copy-start
  82.8 1.6 %copy.10 = bf16[160,384]{1,0:T(8,128)(2,1)} copy(bf16[160,384]{1,0:T(8,128)(2,1)} %get-tuple-element.4) | data formatting | bytes 245760
  84.4 0.0 copy-done
  84.4 0.6 copy.11
Async XLA Ops:
  82.8 1.6 %copy-start = (bf16[32,384]{1,0:T(8,128)(2,1)S(1)}, bf16[32,384]{1,0:T(8,128)(2,1)}, u32[]{:S(2)}) copy-start(bf16[32,384]{1,0:T(8,128)(2,1)} %get-tuple-element.5) | copy-start | bytes 73732

commit v7 on v5

--- a/solution.py
+++ b/solution.py
@@ -96,7 +96,7 @@
 
     exchanges = (
         (dq_arg, dq_parts), (k_arg, k_parts), (v_arg, v_parts),
-        (q_arg, q_parts), (ck_arg, ck_parts), (cv_arg, cv_parts),
+        (ck_arg, ck_parts), (cv_arg, cv_parts), (q_arg, q_parts),
     )
 
     def slab(which, peer):
@@ -249,19 +249,19 @@
     query_hop(1)
     hop(1)
     query_hop(2)
-    place(3, qb.at[0])
-    send(qb.at[0], qb.at[1], ms.at[1], mr.at[1], mirror)
+    place(3, ckb.at[0])
+    send(ckb.at[0], ckb.at[1], ms.at[2], mr.at[2], twin)
+    place(4, cvb.at[0])
+    send(cvb.at[0], cvb.at[1], ms.at[3], mr.at[3], twin)
     hop(2)
     query_hop(3)
-    place(4, ckb.at[0])
-    send(ckb.at[0], ckb.at[1], ms.at[2], mr.at[2], twin)
-    place(5, cvb.at[0])
-    send(cvb.at[0], cvb.at[1], ms.at[3], mr.at[3], twin)
-    hop(3)
+    place(5, qb.at[0])
+    send(qb.at[0], qb.at[1], ms.at[1], mr.at[1], mirror)
     query_hop(4)
     arrived(ckb.at[1], mr.at[2])
     arrived(cvb.at[1], mr.at[3])
     visit_all()
+    hop(3)
     arrived(qb.at[1], mr.at[1])
     from_twin(0)
     attend(both, (0,), True)

time: 82.6 us -> 85.9 us (1.040)
  Pallas kernels: 79.6 us -> 82.9 us
    pallas_call x1, Pallas kernels: 79.6 us -> 82.9 us  [attention(): pl.pallas_call(kernel, out_shape=(jax.ShapeDtypeStruct((rows, columns), b...]
where the time goes in v7:
time: 85.9 us; the launch traced here: 85.7 us
  Pallas kernels  82.9 us (97%)
  local copies, waits for them, and re-layouts  2.18 us (3%)
    pallas_call x1, Pallas kernels, attention(): pl.pallas_call(kernel, out_shape=(jax.ShapeDtypeStruct((rows, columns), b...  82.9 us
    unnamed x4, local copies, waits for them, and re-layouts  2.18 us

profile of v7, /device:TPU:1, one launch (start us, length us, event | category | flops | bytes accessed | tf_op | source)
XLA Modules:
  0.0 85.7 jit_solution(9357602856520416853)
XLA Ops:
  0.6 82.9 %shard_map.77 = (bf16[160,384]{1,0:T(8,128)(2,1)}, bf16[32,384]{1,0:T(8,128)(2,1)}) custom-call(bf16[10,6144]{1,0:T(8,128)(2,1)} %q_arg.1, bf16[10,6144]{1,0:T(8,128)(2,1)} %k_arg.1, bf16[10,6144]{1,0:T(8,128)(2,1)} %v_arg.1, bf16[2,6144]{1,0:T(2,128)(2,1)} %dq_arg.1, bf16[10,6144]{1,0:T(8,128)(2,1)} %ck_arg.1, bf16[10,6144]{1,0:T(8,128)(2,1)} %cv_arg.1), custom_call_target="tpu_custom_call" | custom-call | tf_op jit(solution)/shard_map/pallas_call | solution.py:369
  83.5 0.0 copy-start
  83.5 1.6 %copy.10 = bf16[160,384]{1,0:T(8,128)(2,1)} copy(bf16[160,384]{1,0:T(8,128)(2,1)} %get-tuple-element.4) | data formatting | bytes 245760
  85.1 0.0 copy-done
  85.1 0.6 copy.11
Async XLA Ops:
  83.5 1.6 %copy-start = (bf16[32,384]{1,0:T(8,128)(2,1)S(1)}, bf16[32,384]{1,0:T(8,128)(2,1)}, u32[]{:S(2)}) copy-start(bf16[32,384]{1,0:T(8,128)(2,1)} %get-tuple-element.5) | copy-start | bytes 73732

commit v8 on v5

--- a/solution.py
+++ b/solution.py
@@ -269,24 +269,9 @@
     attend(both, (1, 7))
     from_twin(2, 6)
     attend(both, (2, 6))
+    hop(4)
     from_twin(3, 5)
     attend(both, (3, 5))
-    hop(4)
-    from_twin(4)
-    attend(mirror_rows, (4,))
-
-    lane = lax.broadcasted_iota(jnp.int32, (rows, HEAD_DIM), 1)
-    held = jnp.zeros((rows, HEAD_DIM), jnp.float32)
-    for head in range(heads):
-        esend[:, head * HEAD_DIM : (head + 1) * HEAD_DIM] = acc[head, mirror_rows].astype(jnp.bfloat16)
-        held = jnp.where(lane == head, top[head, mirror_rows], held)
-        held = jnp.where(lane == heads + head, total[head, mirror_rows], held)
-    estat[0:rows, :] = held
-    for chunk in range(2):
-        esend_stat[chunk] = jnp.transpose(estat[chunk * 128 : (chunk + 1) * 128, :])[0:8]
-    send(esend, eback, ms.at[4], mr.at[4], mirror)
-    send(esend_stat, eback_stat, ms.at[5], mr.at[5], mirror)
-    attend(own_rows, (4,))
 
     for slot in range(1, RING):
         arrived(pback.at[slot], rr.at[slot])
@@ -314,21 +299,21 @@
     send(zsend, zback, ms.at[6], mr.at[6], mirror)
     send(zsend_stat, zback_stat, ms.at[7], mr.at[7], mirror)
 
-    arrived(eback, mr.at[4])
-    arrived(eback_stat, mr.at[5])
-    wide[8:, :] = jnp.zeros((120, 128), jnp.float32)
+    from_twin(4)
+    attend(mirror_rows, (4,))
+
+    lane = lax.broadcasted_iota(jnp.int32, (rows, HEAD_DIM), 1)
+    held = jnp.zeros((rows, HEAD_DIM), jnp.float32)
+    for head in range(heads):
+        esend[:, head * HEAD_DIM : (head + 1) * HEAD_DIM] = acc[head, mirror_rows].astype(jnp.bfloat16)
+        held = jnp.where(lane == head, top[head, mirror_rows], held)
+        held = jnp.where(lane == heads + head, total[head, mirror_rows], held)
+    estat[0:rows, :] = held
     for chunk in range(2):
-        wide[0:8, :] = eback_stat[chunk]
-        estat[chunk * 128 : (chunk + 1) * 128, :] = jnp.transpose(wide[...])
-    for head in range(heads):
-        span = slice(head * HEAD_DIM, (head + 1) * HEAD_DIM)
-        other_top = estat[0:rows, head : head + 1]
-        other_total = estat[0:rows, heads + head : heads + head + 1]
-        peak = jnp.maximum(top[head, own_rows], other_top)
-        mine = jnp.exp2((top[head, own_rows] - peak) * STEEP)
-        theirs = jnp.exp2((other_top - peak) * STEEP)
-        whole = mine * acc[head, own_rows] + theirs * eback[:, span].astype(jnp.float32)
-        enc_ref[:, span] = (whole / (mine * total[head, own_rows] + theirs * other_total)).astype(jnp.bfloat16)
+        esend_stat[chunk] = jnp.transpose(estat[chunk * 128 : (chunk + 1) * 128, :])[0:8]
+    send(esend, eback, ms.at[4], mr.at[4], mirror)
+    send(esend_stat, eback_stat, ms.at[5], mr.at[5], mirror)
+    attend(own_rows, (4,))
 
     arrived(zback, mr.at[6])
     arrived(zback_stat, mr.at[7])
@@ -346,6 +331,22 @@
         theirs = jnp.exp2((other_top - peak) * STEEP)
         whole = mine * dmix[0:drows, span] + theirs * zback[:, span].astype(jnp.float32)
         dec_ref[:, span] = (whole / (mine * own_total + theirs * other_total)).astype(jnp.bfloat16)
+
+    arrived(eback, mr.at[4])
+    arrived(eback_stat, mr.at[5])
+    wide[8:, :] = jnp.zeros((120, 128), jnp.float32)
+    for chunk in range(2):
+        wide[0:8, :] = eback_stat[chunk]
+        estat[chunk * 128 : (chunk + 1) * 128, :] = jnp.transpose(wide[...])
+    for head in range(heads):
+        span = slice(head * HEAD_DIM, (head + 1) * HEAD_DIM)
+        other_top = estat[0:rows, head : head + 1]
+        other_total = estat[0:rows, heads + head : heads + head + 1]
+        peak = jnp.maximum(top[head, own_rows], other_top)
+        mine = jnp.exp2((top[head, own_rows] - peak) * STEEP)
+        theirs = jnp.exp2((other_top - peak) * STEEP)
+        whole = mine * acc[head, own_rows] + theirs * eback[:, span].astype(jnp.float32)
+        enc_ref[:, span] = (whole / (mine * total[head, own_rows] + theirs * other_total)).astype(jnp.bfloat16)
 
     for copy in started:
         copy.wait_send()

time: 82.6 us -> 80.2 us (0.971); the launches traced: 82.5 us -> 79.2 us
  Pallas kernels: 79.6 us -> 76.4 us
    pallas_call x1, Pallas kernels: 79.6 us -> 76.4 us  [attention(): pl.pallas_call(kernel, out_shape=(jax.ShapeDtypeStruct((rows, columns), b...]
where the time goes in v8:
time: 80.2 us; the launch traced here: 79.2 us
  Pallas kernels  76.4 us (95%)
  local copies, waits for them, and re-layouts  2.18 us (3%)
    pallas_call x1, Pallas kernels, attention(): pl.pallas_call(kernel, out_shape=(jax.ShapeDtypeStruct((rows, columns), b...  76.4 us
    unnamed x4, local copies, waits for them, and re-layouts  2.18 us

profile of v8, /device:TPU:1, one launch (start us, length us, event | category | flops | bytes accessed | tf_op | source)
XLA Modules:
  0.0 79.2 jit_solution(14990650899024593626)
XLA Ops:
  0.6 76.4 %shard_map.77 = (bf16[160,384]{1,0:T(8,128)(2,1)}, bf16[32,384]{1,0:T(8,128)(2,1)}) custom-call(bf16[10,6144]{1,0:T(8,128)(2,1)} %q_arg.1, bf16[10,6144]{1,0:T(8,128)(2,1)} %k_arg.1, bf16[10,6144]{1,0:T(8,128)(2,1)} %v_arg.1, bf16[2,6144]{1,0:T(2,128)(2,1)} %dq_arg.1, bf16[10,6144]{1,0:T(8,128)(2,1)} %ck_arg.1, bf16[10,6144]{1,0:T(8,128)(2,1)} %cv_arg.1), custom_call_target="tpu_custom_call" | custom-call | tf_op jit(solution)/shard_map/pallas_call | solution.py:370
  77.0 0.0 copy-start
  77.0 1.6 %copy.10 = bf16[160,384]{1,0:T(8,128)(2,1)} copy(bf16[160,384]{1,0:T(8,128)(2,1)} %get-tuple-element.4) | data formatting | bytes 245760
  78.6 0.0 copy-done
  78.6 0.6 copy.11
Async XLA Ops:
  77.0 1.6 %copy-start = (bf16[32,384]{1,0:T(8,128)(2,1)S(1)}, bf16[32,384]{1,0:T(8,128)(2,1)}, u32[]{:S(2)}) copy-start(bf16[32,384]{1,0:T(8,128)(2,1)} %get-tuple-element.5) | copy-start | bytes 73732
